TPU v7x, 512 devices: a whole 4x4x16 slice. The times are simulated.
512 devices in a mesh: seq: 16 (over z_lo, core), tp: 8 (over z_hi, y), rep: 4 (over x).
Axes of the slice: x: 4, y: 4, z: 16 (z_hi: 2, z_lo: 8; z = z_hi * 8 + z_lo), core: 2. Of those that a mesh axis runs over, the one named last changes fastest.
Arguments:
- counts: int32 [4, 16], P('rep'), may hold values from 1 to 40, 256 in all within a row
- prompt_of: int32 [4, 256], P('rep'), may hold values from 0 to 7, as said below
- queries: bfloat16 [4, 640, 8192], P('rep', 'seq', 'tp'), may hold values from -10 to 10
- new_kv: bfloat16 [4, 640, 2, 1024], P('rep', 'seq', None, 'tp'), may hold values from -10 to 10
- prompt_keys: bfloat16 [4, 8, 16384, 1024], P('rep', None, 'seq', 'tp'), may hold values from -6 to 6
- prompt_values: bfloat16 [4, 8, 16384, 1024], P('rep', None, 'seq', 'tp'), may hold values from -6 to 6
- suffix_keys: bfloat16 [4, 256, 64, 1024], P('rep', 'seq', None, 'tp'), may hold values from -9 to 9
- suffix_values: bfloat16 [4, 256, 64, 1024], P('rep', 'seq', None, 'tp'), may hold values from -6 to 6
- gen_len: int32 [4, 256], P('rep', 'seq'), may hold values from 1 to 64, 8192 in all within a row
- out_weight: bfloat16 [8192, 8192], P('tp', ('seq', 'rep')), may hold values from -0.0625 to 0.0625
Outputs:
- projected: bfloat16 [1024, 8192], P('tp', ('seq', 'rep'))
Inputs may be any that keep to these rules, and one draw needn't show every extreme that they name: In each group the live slots of seq index s are its first counts[s] slots; together they hold the group's rows in order. `prompt_of`: in each group every prompt is named by exactly 32 rows.
All inputs are finite; a program needn't handle non-finite values. No bound on the sum of `gen_len` on one device may be relied on, other than what follows from the above.
Results may differ from a plain program's by a relative error of at most 0.014.
Values may be sent and summed in bfloat16 or wider, within the bound.
No kernel may reach another device: no remote copies, remote signals or barrier semaphores. Data moves between devices by JAX's collectives and lax.ppermute only.
A program may use at most 128 MiB of HBM per device.

v0:
```python
import jax
import jax.numpy as jnp
from jax import lax
from jax.sharding import PartitionSpec as P

HD = 128


def combined_all(value, axis, join):
    pieces = jax.tree.map(lambda part: lax.all_gather(part, axis), value)
    head = jax.tree.map(lambda part: part[0], pieces)
    tail = jax.tree.map(lambda part: part[1:], pieces)
    so_far, _ = lax.scan(lambda so_far, section: (join(so_far, section), None), head, tail)
    return so_far


def softmax_join(first, second):
    peak_a, total_a, mixed_a = first
    peak_b, total_b, mixed_b = second
    joined = jnp.maximum(peak_a, peak_b)
    factor_a = jnp.exp(peak_a - joined)
    factor_b = jnp.exp(peak_b - joined)
    depth = mixed_a.shape[-1] // peak_a.shape[-1]
    mixed = mixed_a * jnp.repeat(factor_a, depth, axis=-1) + mixed_b * jnp.repeat(
        factor_b, depth, axis=-1
    )
    return (joined, total_a * factor_a + total_b * factor_b, mixed)


def body(
    counts,
    prompt_of,
    queries,
    new_kv,
    prompt_keys,
    prompt_values,
    suffix_keys,
    suffix_values,
    gen_len,
    out_weight,
):
    seq_count = lax.axis_size("seq")
    seq_index = lax.axis_index("seq")
    capacity = queries.shape[1]
    width = queries.shape[2]
    kv_width = new_kv.shape[3]
    kv_local = kv_width // HD
    q_local = width // HD
    share = q_local // kv_local
    per_device = gen_len.shape[1]
    group_rows = per_device * seq_count
    prompt_count = prompt_keys.shape[1]
    block_rows = group_rows // prompt_count
    scale = HD ** (-0.5)
    tally = counts[0]
    ends = jnp.cumsum(tally)
    starts = ends - tally
    row_ids = jnp.arange(group_rows, dtype=jnp.int32)
    holder = jnp.sum((ends[None, :] <= row_ids[:, None]).astype(jnp.int32), axis=1)
    devices = jnp.arange(seq_count, dtype=jnp.int32)
    first_row = jnp.sum(jnp.where(holder[:, None] == devices[None, :], starts[None, :], 0), axis=1)
    slot_of_row = holder * capacity + row_ids - first_row
    slot_queries, slot_kv = (
        lax.all_gather(queries[0], "seq", axis=0, tiled=True),
        lax.all_gather(new_kv[0].reshape(capacity, 2 * kv_width), "seq", axis=0, tiled=True),
    )
    picker = (
        slot_of_row[:, None] == jnp.arange(seq_count * capacity, dtype=jnp.int32)[None, :]
    ).astype(jnp.bfloat16)
    row_queries = jnp.dot(picker, slot_queries, preferred_element_type=jnp.float32).astype(
        jnp.bfloat16
    )
    own_picker = lax.dynamic_slice_in_dim(picker, seq_index * per_device, per_device, 0)
    own_kv = jnp.dot(own_picker, slot_kv, preferred_element_type=jnp.float32).astype(jnp.bfloat16)
    grouped = row_queries.reshape(group_rows, kv_local, share, HD)
    row_order = jnp.argsort(prompt_of[0], stable=True)

    def prompt_step(index, carry):
        best, total, mixed = carry
        rows = lax.dynamic_slice_in_dim(row_order, index * block_rows, block_rows, 0)
        block_queries = jnp.take(grouped, rows, axis=0)
        keys = lax.dynamic_index_in_dim(prompt_keys[0], index, 0, keepdims=False).reshape(
            -1, kv_local, HD
        )
        values = lax.dynamic_index_in_dim(prompt_values[0], index, 0, keepdims=False).reshape(
            -1, kv_local, HD
        )
        scores = (
            jnp.einsum("rkgd,nkd->rkgn", block_queries, keys, preferred_element_type=jnp.float32)
            * scale
        )
        peak = jnp.max(scores, axis=-1)
        weights = jnp.exp(scores - peak[..., None])
        mass = jnp.sum(weights, axis=-1)
        blended = jnp.einsum(
            "rkgn,nkd->rkgd",
            weights.astype(jnp.bfloat16),
            values,
            preferred_element_type=jnp.float32,
        )
        best = best.at[rows].set(peak.reshape(block_rows, q_local))
        total = total.at[rows].set(mass.reshape(block_rows, q_local))
        mixed = mixed.at[rows].set(blended.reshape(block_rows, width))
        return (best, total, mixed)

    start_state = (
        jnp.zeros((group_rows, q_local), jnp.float32),
        jnp.zeros((group_rows, q_local), jnp.float32),
        jnp.zeros((group_rows, width), jnp.float32),
    )
    partial_value = lax.fori_loop(0, prompt_count, prompt_step, start_state)
    best_all, total_all, mixed_all = combined_all(partial_value, "seq", softmax_join)
    first = seq_index * per_device
    best = lax.dynamic_slice_in_dim(best_all, first, per_device, 0)
    total = lax.dynamic_slice_in_dim(total_all, first, per_device, 0)
    mixed = lax.dynamic_slice_in_dim(mixed_all, first, per_device, 0)
    mine = lax.dynamic_slice_in_dim(row_queries, seq_index * per_device, per_device, 0).reshape(
        per_device, kv_local, share, HD
    )
    cache_keys = suffix_keys[0].reshape(per_device, -1, kv_local, HD)
    cache_values = suffix_values[0].reshape(per_device, -1, kv_local, HD)
    suffix_scores = (
        jnp.einsum("rkgd,rskd->rkgs", mine, cache_keys, preferred_element_type=jnp.float32) * scale
    )
    live = jnp.arange(cache_keys.shape[1], dtype=jnp.int32)[None, :] < gen_len[0][:, None]
    suffix_scores = jnp.where(live[:, None, None, :], suffix_scores, -jnp.inf)
    fresh_keys = own_kv[:, :kv_width].reshape(per_device, kv_local, HD)
    fresh_values = own_kv[:, kv_width:].reshape(per_device, kv_local, HD)
    self_score = (
        jnp.einsum("rkgd,rkd->rkg", mine, fresh_keys, preferred_element_type=jnp.float32) * scale
    )
    prior = best.reshape(per_device, kv_local, share)
    peak = jnp.maximum(jnp.maximum(prior, jnp.max(suffix_scores, axis=-1)), self_score)
    carry_factor = jnp.exp(prior - peak)
    suffix_weights = jnp.exp(suffix_scores - peak[..., None])
    self_weight = jnp.exp(self_score - peak)
    mass = (
        total.reshape(per_device, kv_local, share) * carry_factor
        + jnp.sum(suffix_weights, axis=-1)
        + self_weight
    )
    blended = mixed.reshape(per_device, kv_local, share, HD) * carry_factor[..., None]
    blended = blended + jnp.einsum(
        "rkgs,rskd->rkgd",
        suffix_weights.astype(jnp.bfloat16),
        cache_values,
        preferred_element_type=jnp.float32,
    )
    blended = (
        blended
        + self_weight.astype(jnp.bfloat16).astype(jnp.float32)[..., None]
        * fresh_values.astype(jnp.float32)[:, :, None, :]
    )
    attended = (blended / mass[..., None]).reshape(per_device, width).astype(jnp.bfloat16)
    group_block = lax.all_gather(attended, "seq", axis=0, tiled=True)
    every_row = lax.all_gather(group_block, "rep", axis=0, tiled=True)
    summed = lax.psum_scatter(
        jnp.dot(every_row, out_weight, preferred_element_type=jnp.float32).astype(jnp.bfloat16),
        "tp",
        scatter_dimension=0,
        tiled=True,
    )
    return summed


def solution(mesh):
    in_specs = (
        P("rep", None),
        P("rep", None),
        P("rep", "seq", "tp"),
        P("rep", "seq", None, "tp"),
        P("rep", None, "seq", "tp"),
        P("rep", None, "seq", "tp"),
        P("rep", "seq", None, "tp"),
        P("rep", "seq", None, "tp"),
        P("rep", "seq"),
        P("tp", ("seq", "rep")),
    )
    out_specs = P("tp", ("seq", "rep"))
    return jax.shard_map(body, mesh=mesh, in_specs=in_specs, out_specs=out_specs, check_vma=False)
```

profile of v0, /device:TPU:6, one launch (start us, length us, event | category | flops | bytes accessed | tf_op | source)
XLA Modules:
  0.0 615.0 jit_solution(17350070838944272448)
XLA Ops:
  8.2 3.8 sort.17
  12.9 99.9 %all-gather.10.cloned.1.call-done = bf16[1,640,1024]{2,1,0:T(8,128)(2,1)} async-done(((bf16[1,40,1024]{2,1,0:T(8,128)(2,1)}), bf16[1,640,1024]{2,1,0:T(8,128)(2,1)}) %all-gather.10.cloned.1.call-update) | async-done | bytes 1310736 | tf_op jit(solution)/shard_map/all_gather | solution.py:64
  115.0 53.4 %while.31 = (s32[]{:T(128)}, f32[256,8]{1,0:T(8,128)S(1)}, f32[256,8]{1,0:T(8,128)S(1)}, f32[256,1024]{1,0:T(8,128)S(1)}, s32[256]{0:T(256)S(1)}, /*index=5*/bf1...) while((s32[]{:T(128)}, f32[256,8]{1,0:T(8,128)S(1)}, ...), condition=%wide.region_10.11_spmd, body=%wide.region_4.10_spmd.sunk | while | flops 135824064 | bytes 5590007 | solution.py:111
  169.5 32.9 %all_gather.37 = bf16[640,256]{1,0:T(8,128)(2,1)S(1)} all-gather(bf16[40,256]{1,0:T(8,128)(2,1)S(1)} %bitcast.160), channel_id=1, replica_groups=mesh['seq'=16,'tp'=8,'rep'=4] {'seq'}, dimensions={0}, use_global_device_ids=true | all-gather | bytes 348160 | tf_op jit(solution)/shard_map/all_gather | solution.py:65
  202.8 27.2 %all-gather.2 = f32[4096,8]{0,1:T(8,128)S(1)} all-gather(f32[256,8]{0,1:T(8,128)S(1)} %copy.54), channel_id=4, replica_groups=mesh['seq'=16,'tp'=8,'rep'=4] {'seq'}, dimensions={0}, use_global_device_ids=true | all-gather | bytes 139264 | tf_op jit(solution)/shard_map/all_gather | solution.py:10
  230.1 29.0 %all-gather.1 = f32[4096,8]{0,1:T(8,128)S(1)} all-gather(f32[256,8]{0,1:T(8,128)S(1)} %copy.53), channel_id=3, replica_groups=mesh['seq'=16,'tp'=8,'rep'=4] {'seq'}, dimensions={0}, use_global_device_ids=true | all-gather | bytes 139264 | tf_op jit(solution)/shard_map/all_gather | solution.py:10
  259.6 107.9 %all-gather.12.cloned.1.call-done = f32[4096,1024]{1,0:T(8,128)} async-done(((f32[256,1024]{1,0:T(8,128)}), f32[4096,1024]{1,0:T(8,128)}) %all-gather.12.cloned.1.call-update) | async-done | bytes 16777232 | tf_op jit(solution)/shard_map/all_gather | solution.py:10
  367.5 14.6 %slice.45 = f32[3840,1024]{1,0:T(8,128)} slice(f32[4096,1024]{1,0:T(8,128)} %all-gather.12.cloned.1.call-done), slice={[256:4096], [0:1024]} | slice | bytes 31457280 | tf_op jit(solution)/shard_map/slice | solution.py:12
  382.1 47.0 %while.32 = (s32[]{:T(128)}, f32[256,8]{0,1:T(8,128)S(1)}, f32[256,8]{0,1:T(8,128)S(1)}, f32[256,1024]{1,0:T(8,128)S(1)}, f32[15,256,8]{1,2,0:T(8,128)S(1)}, /*i...) while((s32[]{:T(128)}, f32[256,8]{0,1:T(8,128)S(1)}, f32[256,8]{0,1:T(8,128)S(1)}, ...), condition=%wide.region_12.13_spmd, body=%wide.region_11.12_spmd.sunk | while | flops 798722 | bytes 7454821 | solution.py:13
  383.0 2.2 fusion.63
  386.2 2.2 fusion.63
  389.3 2.2 fusion.63
  392.4 2.2 fusion.63
  395.6 2.2 fusion.63
  398.7 2.2 fusion.63
  401.8 2.2 fusion.63
  405.0 2.2 fusion.63
  408.1 2.2 fusion.63
  411.2 2.2 fusion.63
  414.4 2.2 fusion.63
  430.0 29.6 %all_gather.38 = bf16[256,1024]{1,0:T(8,128)(2,1)} all-gather(bf16[16,1024]{1,0:T(8,128)(2,1)S(1)} %bitcast.159), channel_id=1, replica_groups=mesh['seq'=16,'tp'=8,'rep'=4] {'seq'}, dimensions={0}, use_global_device_ids=true | all-gather | bytes 557056 | tf_op jit(solution)/shard_map/all_gather | solution.py:155
  459.6 33.2 %all-gather.8.cloned.1.call-done = bf16[1024,1024]{1,0:T(8,128)(2,1)} async-done(((bf16[256,1024]{1,0:T(8,128)(2,1)}), bf16[1024,1024]{1,0:T(8,128)(2,1)}) %all-gather.8.cloned.1.call-update) | async-done | bytes 2097168 | tf_op jit(solution)/shard_map/all_gather | solution.py:156
  492.8 3.0 convolution_convert_fusion
  495.9 112.6 %reduce-scatter.2.cloned.1.call-done = bf16[128,128]{1,0:T(8,128)(2,1)} async-done(((bf16[1024,128]{1,0:T(8,128)(2,1)}), bf16[128,128]{1,0:T(8,128)(2,1)}) %reduce-scatter.2.cloned.1.call-update) | async-done | bytes 32784 | tf_op jit(solution)/shard_map/reduce_scatter | solution.py:157
  (243 shorter events, 83.0 us)
Async XLA Ops:
  6.5 486.3 %copy-start = (bf16[1024,128]{1,0:T(8,128)(2,1)S(1)}, bf16[1024,128]{1,0:T(8,128)(2,1)}, u32[]{:S(2)}) copy-start(bf16[1024,128]{1,0:T(8,128)(2,1)} %param.23) | copy-start | bytes 786436
  6.5 106.2 %all-gather.10.cloned.1.call-start = ((), (), s32[]{:S(2)}) async-start(), calls=%async_computation.3 | async-start | bytes 1392640 | tf_op jit(solution)/shard_map/all_gather | solution.py:64
  7.3 360.2 %all-gather.12.cloned.1.call-start = ((), (), s32[]{:S(2)}) async-start(), calls=%async_computation.4 | async-start | bytes 17825792 | tf_op jit(solution)/shard_map/all_gather | solution.py:10
  115.0 54.5 %copy-start.3 = (bf16[1,40,2,128]{3,2,1,0:T(2,128)(2,1)S(1)}, bf16[1,40,2,128]{3,2,1,0:T(2,128)(2,1)}, u32[]{:S(2)}) copy-start(bf16[1,40,2,128]{3,2,1,0:T(2,128)(2,1)} %param.17) | copy-start | bytes 61444
  115.0 87.4 %copy-start.4 = (s32[1,16]{1,0:T(1,128)S(1)}, s32[1,16]{1,0:T(1,128)}, u32[]{:S(2)}) copy-start(s32[1,16]{1,0:T(1,128)} %param.22) | copy-start | bytes 196
  168.4 1.0 copy-start.1
  168.4 90.9 %copy-start.2 = (bf16[1,16,64,128]{3,2,1,0:T(8,128)(2,1)S(1)}, bf16[1,16,64,128]{3,2,1,0:T(8,128)(2,1)}, u32[]{:S(2)}) copy-start(bf16[1,16,64,128]{3,2,1,0:T(8,128)(2,1)} %param.20) | copy-start | bytes 786436
  169.4 323.5 %all-gather.8.cloned.1.call-start = ((), (), s32[]{:S(2)}) async-start(), calls=%async_computation.1 | async-start | bytes 2621440 | tf_op jit(solution)/shard_map/all_gather | solution.py:156
  367.4 14.6 %slice-start = ((f32[4096,1024]{1,0:T(8,128)}), f32[256,1024]{1,0:T(8,128)S(1)}, s32[]{:S(2)}) async-start(f32[4096,1024]{1,0:T(8,128)} %all-gather.12.cloned.1.call-done), calls=%async_computation.5 | async-start | bytes 2097152 | tf_op jit(solution)/shard_map/slice | solution.py:11
  382.1 47.6 %copy-start.5 = (bf16[1,16,64,128]{3,2,1,0:T(8,128)(2,1)S(1)}, bf16[1,16,64,128]{3,2,1,0:T(8,128)(2,1)}, u32[]{:S(2)}) copy-start(bf16[1,16,64,128]{3,2,1,0:T(8,128)(2,1)} %param.21) | copy-start | bytes 786436
  459.6 148.9 %reduce-scatter.2.cloned.1.call-start = ((), (), s32[]{:S(2)}) async-start(), calls=%async_computation.2 | async-start | bytes 294912 | tf_op jit(solution)/shard_map/reduce_scatter | solution.py:157
Sparse Core Ops, SparseCore 0:
  9.4 103.3 all-gather.9
  169.5 197.9 all-gather.11
  459.7 33.0 all-gather.7
  497.1 111.3 reduce-scatter.1
where the time goes:
time: 616 us; the launch traced here: 615 us
  waiting for transfers between devices  354 us (57%)
  blocking collectives  119 us (19%)
  local copies, waits for them, and re-layouts  58.6 us (10%)
  other arithmetic  41.9 us (7%)
  matrix products  26.8 us (4%)
  between operations  13.4 us (2%)
    reduce_scatter x1, waiting for transfers between devices, body(): lax.psum_scatter(jnp.dot(every_row, out_weight, preferred_element_type=jn...  113 us
    all_gather x1, waiting for transfers between devices, combined_all(): pieces = jax.tree.map(lambda part: lax.all_gather(part, axis), value)  108 us
    all_gather x1, waiting for transfers between devices, body(): lax.all_gather(queries[0], 'seq', axis=0, tiled=True)  99.9 us
    all_gather x2, blocking collectives, combined_all(): pieces = jax.tree.map(lambda part: lax.all_gather(part, axis), value)  56.2 us
    all_gather x1, waiting for transfers between devices, body(): every_row = lax.all_gather(group_block, 'rep', axis=0, tiled=True)  33.2 us
    all_gather x1, blocking collectives, body(): lax.all_gather(new_kv[0].reshape(capacity, 2 * kv_width), 'seq', axis=0,...  32.9 us
    add x15, other arithmetic, softmax_join(): mixed_a * jnp.repeat(factor_a, depth, axis=-1)  32.4 us
    all_gather x1, blocking collectives, body(): group_block = lax.all_gather(attended, 'seq', axis=0, tiled=True)  29.6 us
  transfers between devices with their start and end apart: 4, of which 4 were waited for; matrix products, arithmetic and copies ran while one was open for 1% of the time, Pallas kernels for 0%

commit v1 on v0

v1 whole, which is shorter than its diff:
```python
import functools
import math

import jax
import jax.numpy as jnp
from jax import lax
from jax.experimental import pallas as pl
from jax.experimental.pallas import tpu as pltpu
from jax.sharding import PartitionSpec as P

HD = 128
LANES = 128
NEG = -1e30
BF = jnp.bfloat16
F32 = jnp.float32


def swap(x, axis, bit):
    size = lax.axis_size(axis)
    return lax.ppermute(x, axis, [(i, i ^ bit) for i in range(size)])


def dot(a, b):
    return lax.dot_general(a, b, (((1,), (0,)), ((), ())), preferred_element_type=F32)


def dot_t(a, b):
    return lax.dot_general(a, b, (((1,), (1,)), ((), ())), preferred_element_type=F32)


def split_stats(stat):
    hi = stat.astype(BF).astype(F32)
    rest = stat - hi
    mid = rest.astype(BF).astype(F32)
    low = rest - mid
    lane = lax.broadcasted_iota(jnp.int32, stat.shape, 1)
    out = jnp.where(lane < 8, hi, jnp.where(lane < 16, pltpu.roll(mid, 8, 1), pltpu.roll(low, 16, 1)))
    return jnp.where(lane < 24, out, 0.0).astype(BF)


def join_stats(packed):
    x = packed.astype(F32)
    return x + pltpu.roll(x, LANES - 8, 1) + pltpu.roll(x, LANES - 16, 1)


def heads_down(x, heads):
    return jnp.concatenate([x[:, h * HD : (h + 1) * HD] for h in range(heads)], axis=0)


def lanes_of(column, heads, rows):
    lane = lax.broadcasted_iota(jnp.int32, (rows, LANES), 1)
    out = jnp.zeros((rows, LANES), F32)
    for h in range(heads):
        out = jnp.where(lane == h, column[h * rows : (h + 1) * rows], out)
    return out


def one_hot(ids, width, offset=0):
    lane = lax.broadcasted_iota(jnp.int32, (ids.shape[0], width), 1)
    return jnp.where(ids - offset == lane, 1.0, 0.0).astype(BF)


def attend_kernel(heads, scalars, spos, dest, own_pos, gens, near, far, new_k, new_v, keys, values, suf_k, suf_v, keep, send, sorted_rows):
    step = pl.program_id(0)
    width = heads * HD
    half = near.shape[0]
    factor = HD**-0.5 * math.log2(math.e)

    def pick(ids):
        q = dot(one_hot(ids, half), near[...]) + dot(one_hot(ids, half, half), far[...])
        return heads_down(q.astype(BF), heads)

    ids = spos[...]
    rows = ids.shape[0]
    q = pick(ids)
    fresh = one_hot(ids, new_k.shape[0])
    fresh_k = jnp.concatenate([dot(fresh, new_k[...])] * heads, axis=0)
    fresh_v = jnp.concatenate([dot(fresh, new_v[...])] * heads, axis=0)
    mine = jnp.concatenate([ids] * heads, axis=0) < new_k.shape[0]
    self_score = jnp.sum(q.astype(F32) * fresh_k, axis=1, keepdims=True)
    self_score = jnp.where(mine, self_score, NEG)
    scores = dot_t(q, keys[0])
    peak = jnp.maximum(jnp.max(scores, axis=1, keepdims=True), self_score)
    weights = jnp.exp2((scores - peak) * factor)
    self_weight = jnp.exp2((self_score - peak) * factor)
    mass = jnp.sum(weights, axis=1, keepdims=True) + self_weight
    mixed = dot(weights.astype(BF), values[0]) + self_weight.astype(BF).astype(F32) * fresh_v
    mixed = (mixed / mass).astype(BF)
    at = pl.ds(pl.multiple_of(step * rows, rows), rows)
    for h in range(heads):
        sorted_rows[at, h * HD : (h + 1) * HD] = mixed[h * rows : (h + 1) * rows]
    stat = lanes_of(peak * factor + jnp.log2(mass), heads, rows)
    sorted_rows[at, width : width + LANES] = split_stats(stat)

    @pl.when(step == pl.num_programs(0) - 1)
    def _():
        total = sorted_rows.shape[0]
        place = lax.broadcasted_iota(jnp.int32, (total, total), 0)
        to_dest = jnp.where(place == dest[...], 1.0, 0.0).astype(BF)
        placed = dot(to_dest, sorted_rows[...]).astype(BF)
        keep[...] = placed[: total // 2]
        send[...] = placed[total // 2 :]
        own = own_pos.shape[0]
        qs = pick(own_pos[...])
        suffix = dot_t(qs, suf_k[...])
        depth = suf_k.shape[0] // own
        row = lax.broadcasted_iota(jnp.int32, suffix.shape, 0) % own
        col = lax.broadcasted_iota(jnp.int32, suffix.shape, 1)
        length = jnp.concatenate([gens[...]] * heads, axis=0)
        live = (col // depth == row) & (col % depth < length)
        suffix = jnp.where(live, suffix, NEG)
        top = jnp.max(suffix, axis=1, keepdims=True)
        w = jnp.where(live, jnp.exp2((suffix - top) * factor), 0.0)
        m = jnp.sum(w, axis=1, keepdims=True)
        o = dot(w.astype(BF), suf_v[...]) / m
        stat_s = lanes_of(top * factor + jnp.log2(m), heads, own)
        here = pl.ds(pl.multiple_of(scalars[0], own), own)
        old = keep[here, :]
        stat_p = join_stats(old[:, width : width + LANES])
        both = jnp.maximum(stat_p, stat_s)
        e_p, e_s = jnp.exp2(stat_p - both), jnp.exp2(stat_s - both)
        t = e_p + e_s
        f_p, f_s = e_p / t, e_s / t
        for h in range(heads):
            cut = slice(h * HD, (h + 1) * HD)
            keep[here, cut] = (
                old[:, cut].astype(F32) * f_p[:, h : h + 1] + o[h * own : (h + 1) * own] * f_s[:, h : h + 1]
            ).astype(BF)
        keep[here, width : width + LANES] = split_stats(both + jnp.log2(t))


def join_kernel(heads, parts, last, *refs):
    a, b = refs[:2]
    outs = refs[2:]
    width = heads * HD
    sa = join_stats(a[:, width : width + LANES])
    sb = join_stats(b[:, width : width + LANES])
    both = jnp.maximum(sa, sb)
    ea, eb = jnp.exp2(sa - both), jnp.exp2(sb - both)
    t = ea + eb
    fa, fb = ea / t, eb / t
    n = a.shape[0] // parts
    for h in range(heads):
        cut = slice(h * HD, (h + 1) * HD)
        o = (a[:, cut].astype(F32) * fa[:, h : h + 1] + b[:, cut].astype(F32) * fb[:, h : h + 1]).astype(BF)
        for i in range(parts):
            outs[i][:, cut] = o[i * n : (i + 1) * n]
    if not last:
        packed = split_stats(both + jnp.log2(t))
        for i in range(parts):
            outs[i][:, width : width + LANES] = packed[i * n : (i + 1) * n]


def join(a, b, heads, parts=1, last=False):
    n = a.shape[0] // parts
    cols = heads * HD if last else a.shape[1]
    return pl.pallas_call(
        functools.partial(join_kernel, heads, parts, last),
        out_shape=[jax.ShapeDtypeStruct((n, cols), BF)] * parts,
        in_specs=[pl.BlockSpec(memory_space=pltpu.VMEM)] * 2,
        out_specs=[pl.BlockSpec(memory_space=pltpu.VMEM)] * parts,
        name="join",
    )(a, b)


def project_kernel(groups, own, scalars, mine, other, weight, out):
    z_bit, core = scalars[1], scalars[2]
    for rel, ref in ((0, mine), (1, other)):
        y = dot(ref[...], weight[...]).astype(BF)
        at = 0
        for g in range(groups):
            for z_rel in range(2):
                for high in range(2):
                    for mid in range(2):
                        block = mid * 4 + (z_bit ^ z_rel) * 2 + (core ^ rel)
                        out[2 * g + high, block] = y[at : at + own]
                        at += own


def body(counts, prompt_of, queries, new_kv, prompt_keys, prompt_values, suffix_keys, suffix_values, gen_len, out_weight):
    me = lax.axis_index("seq")
    capacity, width = queries.shape[1:]
    heads = width // HD
    per_device = gen_len.shape[1]
    seq_count = lax.axis_size("seq")
    total = per_device * seq_count
    prompts, depth = prompt_keys.shape[1:3]
    block = total // prompts
    groups = lax.axis_size("rep")

    slots = queries[0]
    for bit in (8, 4, 2):
        slots = jnp.concatenate([slots, swap(slots, "seq", bit)], axis=0)
    others = swap(slots, "seq", 1)

    tally = counts[0]
    ends = jnp.cumsum(tally)
    row = jnp.arange(total, dtype=jnp.int32)
    past = ends[None, :] <= row[:, None]
    holder = jnp.sum(past.astype(jnp.int32), axis=1)
    offset = row - jnp.sum(jnp.where(past, tally[None, :], 0), axis=1)
    far = holder ^ me
    slot = (((far >> 3) & 1) + ((far >> 2) & 1) * 2 + ((far >> 1) & 1) * 4 + (far & 1) * 8) * capacity + offset
    device = row // per_device
    away = device ^ me
    dest = (
        (away & 1) * (total // 2)
        + ((away >> 1) & 1) * (total // 4)
        + (((device >> 2) & 1) + ((device >> 3) & 1) * 2) * per_device
        + row % per_device
    )
    prompt = prompt_of[0]
    before = (prompt[None, :] == prompt[:, None]) & (row[None, :] < row[:, None])
    rank = prompt * block + jnp.sum(before.astype(jnp.int32), axis=1)
    at_rank = rank[None, :] == row[:, None]
    slot_sorted = jnp.sum(jnp.where(at_rank, slot[None, :], 0), axis=1)
    dest_sorted = jnp.sum(jnp.where(at_rank, dest[None, :], 0), axis=1)
    own_slot = lax.dynamic_slice_in_dim(slot, me * per_device, per_device, 0)
    own_place = (((me >> 2) & 1) + ((me >> 3) & 1) * 2) * per_device
    scalars = jnp.stack([own_place, (me >> 1) & 1, me & 1, me]).astype(jnp.int32)

    packed = width + LANES
    half = slots.shape[0]
    whole = lambda *shape: pl.BlockSpec(shape, lambda i, s: (0,) * len(shape))
    keep, send = pl.pallas_call(
        functools.partial(attend_kernel, heads),
        out_shape=[jax.ShapeDtypeStruct((total // 2, packed), BF)] * 2,
        grid_spec=pltpu.PrefetchScalarGridSpec(
            num_scalar_prefetch=1,
            grid=(prompts,),
            in_specs=[
                pl.BlockSpec((block, 1), lambda i, s: (i, 0)),
                whole(1, total),
                whole(per_device, 1),
                whole(per_device, 1),
                whole(half, width),
                whole(half, width),
                whole(capacity, HD),
                whole(capacity, HD),
                pl.BlockSpec((1, depth, HD), lambda i, s: (i, 0, 0)),
                pl.BlockSpec((1, depth, HD), lambda i, s: (i, 0, 0)),
                whole(per_device * suffix_keys.shape[2], HD),
                whole(per_device * suffix_keys.shape[2], HD),
            ],
            out_specs=[whole(total // 2, packed)] * 2,
            scratch_shapes=[pltpu.VMEM((total, packed), BF)],
        ),
        name="attend",
    )(
        scalars,
        slot_sorted[:, None],
        dest_sorted[None, :],
        own_slot[:, None],
        gen_len[0][:, None],
        slots,
        others,
        new_kv[0, :, 0],
        new_kv[0, :, 1],
        prompt_keys[0],
        prompt_values[0],
        suffix_keys[0].reshape(-1, HD),
        suffix_values[0].reshape(-1, HD),
    )
    keep, send = join(keep, swap(send, "seq", 1), heads, parts=2)
    (part,) = join(keep, swap(send, "seq", 2), heads)
    (part,) = join(part, swap(part, "seq", 4), heads)
    (attended,) = join(part, swap(part, "seq", 8), heads, last=True)
    attended = jnp.concatenate([attended, swap(attended, "seq", 2)], axis=0)
    spread = jnp.broadcast_to(attended[None], (groups,) + attended.shape)
    every = lax.all_to_all(spread, "rep", 0, 0, tiled=True).reshape(-1, width)
    partner = swap(every, "seq", 1)
    tp = lax.axis_size("tp")
    partial_sums = pl.pallas_call(
        functools.partial(project_kernel, groups, per_device),
        out_shape=jax.ShapeDtypeStruct((tp, total // 2 // per_device, per_device, out_weight.shape[1]), BF),
        in_specs=[pl.BlockSpec(memory_space=pltpu.SMEM)] + [pl.BlockSpec(memory_space=pltpu.VMEM)] * 3,
        out_specs=pl.BlockSpec(memory_space=pltpu.VMEM),
        name="project",
    )(scalars, every, partner, out_weight)
    gathered = lax.all_to_all(partial_sums, "tp", 0, 0, tiled=True)
    summed = jnp.sum(gathered.astype(F32), axis=0).astype(BF)
    return summed.reshape(-1, out_weight.shape[1])


def solution(mesh):
    in_specs = (
        P("rep", None),
        P("rep", None),
        P("rep", "seq", "tp"),
        P("rep", "seq", None, "tp"),
        P("rep", None, "seq", "tp"),
        P("rep", None, "seq", "tp"),
        P("rep", "seq", None, "tp"),
        P("rep", "seq", None, "tp"),
        P("rep", "seq"),
        P("tp", ("seq", "rep")),
    )
    out_specs = P("tp", ("seq", "rep"))
    return jax.shard_map(body, mesh=mesh, in_specs=in_specs, out_specs=out_specs, check_vma=False)
```

time: 616 us -> 186 us (0.30)
  the two profiles are of different devices: /device:TPU:6 before, /device:TPU:32 now
where the time goes in v1:
time: 186 us; the launch traced here: 185 us
  blocking collectives  55.9 us (30%)
  starting transfers between devices  46.2 us (25%)
  waiting for transfers between devices  41.9 us (23%)
  Pallas kernels  24.3 us (13%)
  local copies, waits for them, and re-layouts  8.9 us (5%)
  other arithmetic  8.14 us (4%)
    ppermute x10, starting transfers between devices, swap(): return lax.ppermute(x, axis, [(i, i ^ bit) for i in range(size)])  46.2 us
    ppermute x10, waiting for transfers between devices, swap(): return lax.ppermute(x, axis, [(i, i ^ bit) for i in range(size)])  41.9 us
    all_to_all x1, blocking collectives, body(): gathered = lax.all_to_all(partial_sums, 'tp', 0, 0, tiled=True)  37.3 us
    all_to_all x1, blocking collectives, body(): every = lax.all_to_all(spread, 'rep', 0, 0, tiled=True).reshape(-1, width)  18.6 us
    pallas_call x1, Pallas kernels, body(): pl.pallas_call(functools.partial(attend_kernel, heads), out_shape=[jax.Sh...  13.1 us
    pallas_call x4, Pallas kernels, join(): pl.pallas_call(functools.partial(join_kernel, heads, parts, last), out_sh...  8.12 us
    unnamed x18, local copies, waits for them, and re-layouts  4.52 us
  transfers between devices with their start and end apart: 10, of which 9 were waited for; matrix products, arithmetic and copies ran while one was open for 4% of the time, Pallas kernels for 0%

profile of v1, /device:TPU:32, one launch (start us, length us, event | category | flops | bytes accessed | tf_op | source)
XLA Modules:
  0.0 185.5 jit_solution(1329987193553546209)
XLA Ops:
  0.0 9.2 %collective-permute-start = (bf16[40,1024]{1,0:T(8,128)(2,1)}, bf16[40,1024]{1,0:T(8,128)(2,1)S(1)}, u32[]{:S(2)}, u32[]{:S(2)}) collective-permute-start(bf16[40,1024]{1,0:T(8,128)(2,1)} %bitcast.29), channel_id=1, source_target_pairs={{0,256},{32,288},{64,320},{96,352},{128,384},{160,416},{192,448},{... | collective-permute-start | bytes 245768 | tf_op jit(solution)/shard_map/ppermute | solution.py:20
  10.9 4.6 %collective-permute-done = bf16[40,1024]{1,0:T(8,128)(2,1)S(1)} collective-permute-done((bf16[40,1024]{1,0:T(8,128)(2,1)}, bf16[40,1024]{1,0:T(8,128)(2,1)S(1)}, u32[]{:S(2)}, u32[]{:S(2)}) %collective-permute-start) | collective-permute-done | bytes 81952 | tf_op jit(solution)/shard_map/ppermute | solution.py:20
  16.4 4.8 %collective-permute-start.1 = (bf16[80,1024]{1,0:T(8,128)(2,1)S(1)}, bf16[80,1024]{1,0:T(8,128)(2,1)S(1)}, u32[]{:S(2)}, u32[]{:S(2)}) collective-permute-start(bf16[80,1024]{1,0:T(8,128)(2,1)S(1)} %pad_maximum_fusion.3), channel_id=1, source_target_pairs={{0,128},{32,160},{64,192},{96,224},{128,0},{160,32},{192,64},{224,... | collective-permute-start | bytes 491528 | tf_op jit(solution)/shard_map/ppermute | solution.py:20
  23.3 3.3 %collective-permute-done.1 = bf16[80,1024]{1,0:T(8,128)(2,1)S(1)} collective-permute-done((bf16[80,1024]{1,0:T(8,128)(2,1)S(1)}, bf16[80,1024]{1,0:T(8,128)(2,1)S(1)}, u32[]{:S(2)}, u32[]{:S(2)}) %collective-permute-start.1) | collective-permute-done | bytes 163872 | tf_op jit(solution)/shard_map/ppermute | solution.py:20
  27.5 4.1 %collective-permute-start.2 = (bf16[160,1024]{1,0:T(8,128)(2,1)S(1)}, bf16[160,1024]{1,0:T(8,128)(2,1)S(1)}, u32[]{:S(2)}, u32[]{:S(2)}) collective-permute-start(bf16[160,1024]{1,0:T(8,128)(2,1)S(1)} %pad_maximum_fusion.1), channel_id=1, source_target_pairs={{0,64},{32,96},{64,0},{96,32},{128,192},{160,224},{192,128},{224,1... | collective-permute-start | bytes 983048 | tf_op jit(solution)/shard_map/ppermute | solution.py:20
  33.2 5.8 %collective-permute-done.2 = bf16[160,1024]{1,0:T(8,128)(2,1)S(1)} collective-permute-done((bf16[160,1024]{1,0:T(8,128)(2,1)S(1)}, bf16[160,1024]{1,0:T(8,128)(2,1)S(1)}, u32[]{:S(2)}, u32[]{:S(2)}) %collective-permute-start.2) | collective-permute-done | bytes 327712 | tf_op jit(solution)/shard_map/ppermute | solution.py:20
  45.6 13.1 %attend.1 = (bf16[128,1152]{1,0:T(8,128)(2,1)}, bf16[128,1152]{1,0:T(8,128)(2,1)}) custom-call(s32[4]{0:T(128)} %pad_add_fusion.scalars, s32[256,1]{1,0:T(8,128)} %copy.25.spos, s32[1,256]{1,0:T(1,128)} %bitcast.36, s32[16,1]{1,0:T(8,128)} %copy.26.own_pos, s32[16,1]{1,0:T(8,128)} %copy.27.gens, bf16[320,1024]{1,0:T(8,128)(2,1)} %copy-done.1, ...), custom_call_target="tpu_custom_call" | custom-call | tf_op jit(solution)/shard_map/attend/pallas_call | solution.py:225
  58.7 2.4 %collective-permute-start.4 = (bf16[128,1152]{1,0:T(8,128)(2,1)}, bf16[128,1152]{1,0:T(8,128)(2,1)S(1)}, u32[]{:S(2)}, u32[]{:S(2)}) collective-permute-start(bf16[128,1152]{1,0:T(8,128)(2,1)} %get-tuple-element.10), channel_id=1, source_target_pairs={{0,32},{32,0},{64,96},{96,64},{128,160},{160,128},{192,224},{224,1... | collective-permute-start | bytes 884744 | tf_op jit(solution)/shard_map/ppermute | solution.py:20
  63.2 2.2 %join.4 = (bf16[64,1152]{1,0:T(8,128)(2,1)}, bf16[64,1152]{1,0:T(8,128)(2,1)}) custom-call(bf16[128,1152]{1,0:T(8,128)(2,1)} %get-tuple-element.9.refs_0_, bf16[128,1152]{1,0:T(8,128)(2,1)} %copy-done.4), custom_call_target="tpu_custom_call" | custom-call | tf_op jit(solution)/shard_map/join/pallas_call | solution.py:157
  65.5 2.2 %collective-permute-start.5 = (bf16[64,1152]{1,0:T(8,128)(2,1)}, bf16[64,1152]{1,0:T(8,128)(2,1)S(1)}, u32[]{:S(2)}, u32[]{:S(2)}) collective-permute-start(bf16[64,1152]{1,0:T(8,128)(2,1)} %get-tuple-element.12), channel_id=1, source_target_pairs={{0,64},{32,96},{64,0},{96,32},{128,192},{160,224},{192,128},{224,1... | collective-permute-start | bytes 442376 | tf_op jit(solution)/shard_map/ppermute | solution.py:20
  67.6 6.0 %collective-permute-done.5.refs_1_ = bf16[64,1152]{1,0:T(8,128)(2,1)S(1)} collective-permute-done((bf16[64,1152]{1,0:T(8,128)(2,1)}, bf16[64,1152]{1,0:T(8,128)(2,1)S(1)}, u32[]{:S(2)}, u32[]{:S(2)}) %collective-permute-start.5) | collective-permute-done | bytes 147488 | tf_op jit(solution)/shard_map/ppermute | solution.py:20
  74.3 2.0 %join.5.refs_0_ = bf16[64,1152]{1,0:T(8,128)(2,1)} custom-call(bf16[64,1152]{1,0:T(8,128)(2,1)} %get-tuple-element.11.refs_0_, bf16[64,1152]{1,0:T(8,128)(2,1)} %copy-done.5), custom_call_target="tpu_custom_call" | custom-call | tf_op jit(solution)/shard_map/join/pallas_call | solution.py:157
  76.3 5.3 %collective-permute-start.6 = (bf16[64,1152]{1,0:T(8,128)(2,1)}, bf16[64,1152]{1,0:T(8,128)(2,1)S(1)}, u32[]{:S(2)}, u32[]{:S(2)}) collective-permute-start(bf16[64,1152]{1,0:T(8,128)(2,1)} %join.5.refs_0_), channel_id=1, source_target_pairs={{0,128},{32,160},{64,192},{96,224},{128,0},{160,32},{192,64},{224,... | collective-permute-start | bytes 442376 | tf_op jit(solution)/shard_map/ppermute | solution.py:20
  81.6 6.0 %collective-permute-done.6.refs_1_ = bf16[64,1152]{1,0:T(8,128)(2,1)S(1)} collective-permute-done((bf16[64,1152]{1,0:T(8,128)(2,1)}, bf16[64,1152]{1,0:T(8,128)(2,1)S(1)}, u32[]{:S(2)}, u32[]{:S(2)}) %collective-permute-start.6) | collective-permute-done | bytes 147488 | tf_op jit(solution)/shard_map/ppermute | solution.py:20
  88.2 2.0 %join.6.refs_0_ = bf16[64,1152]{1,0:T(8,128)(2,1)} custom-call(bf16[64,1152]{1,0:T(8,128)(2,1)} %join.5.refs_0_, bf16[64,1152]{1,0:T(8,128)(2,1)} %copy-done.6), custom_call_target="tpu_custom_call" | custom-call | tf_op jit(solution)/shard_map/join/pallas_call | solution.py:157
  90.2 8.2 %collective-permute-start.7 = (bf16[64,1152]{1,0:T(8,128)(2,1)}, bf16[64,1152]{1,0:T(8,128)(2,1)S(1)}, u32[]{:S(2)}, u32[]{:S(2)}) collective-permute-start(bf16[64,1152]{1,0:T(8,128)(2,1)} %join.6.refs_0_), channel_id=1, source_target_pairs={{0,256},{32,288},{64,320},{96,352},{128,384},{160,416},{192,448},{... | collective-permute-start | bytes 442376 | tf_op jit(solution)/shard_map/ppermute | solution.py:20
  98.3 8.5 %collective-permute-done.7.refs_1_ = bf16[64,1152]{1,0:T(8,128)(2,1)S(1)} collective-permute-done((bf16[64,1152]{1,0:T(8,128)(2,1)}, bf16[64,1152]{1,0:T(8,128)(2,1)S(1)}, u32[]{:S(2)}, u32[]{:S(2)}) %collective-permute-start.7) | collective-permute-done | bytes 147488 | tf_op jit(solution)/shard_map/ppermute | solution.py:20
  107.5 1.9 %join.7 = bf16[64,1024]{1,0:T(8,128)(2,1)} custom-call(bf16[64,1152]{1,0:T(8,128)(2,1)} %join.6.refs_0_, bf16[64,1152]{1,0:T(8,128)(2,1)} %copy-done.7), custom_call_target="tpu_custom_call" | custom-call | tf_op jit(solution)/shard_map/join/pallas_call | solution.py:157
  109.4 6.2 %collective-permute-start.8 = (bf16[64,1024]{1,0:T(8,128)(2,1)}, bf16[64,1024]{1,0:T(8,128)(2,1)S(1)}, u32[]{:S(2)}, u32[]{:S(2)}) collective-permute-start(bf16[64,1024]{1,0:T(8,128)(2,1)} %join.7), channel_id=1, source_target_pairs={{0,64},{32,96},{64,0},{96,32},{128,192},{160,224},{192,128},{224,1... | collective-permute-start | bytes 393224 | tf_op jit(solution)/shard_map/ppermute | solution.py:20
  115.6 3.7 %collective-permute-done.8 = bf16[64,1024]{1,0:T(8,128)(2,1)S(1)} collective-permute-done((bf16[64,1024]{1,0:T(8,128)(2,1)}, bf16[64,1024]{1,0:T(8,128)(2,1)S(1)}, u32[]{:S(2)}, u32[]{:S(2)}) %collective-permute-start.8) | collective-permute-done | bytes 131104 | tf_op jit(solution)/shard_map/ppermute | solution.py:20
  120.3 18.6 %all_to_all.10 = bf16[4,128,1024]{2,1,0:T(8,128)(2,1)S(1)} all-to-all(bf16[4,128,1024]{2,1,0:T(8,128)(2,1)S(1)} %broadcast_in_dim.64), channel_id=1, replica_groups=mesh['seq'=16,'tp'=8,'rep'=4] {'rep'}, dimensions={0} | all-to-all | bytes 2097152 | tf_op jit(solution)/shard_map/all_to_all | solution.py:270
  140.8 2.6 %collective-permute-done.9.other = bf16[512,1024]{1,0:T(8,128)(2,1)S(1)} collective-permute-done((bf16[512,1024]{1,0:T(8,128)(2,1)S(1)}, bf16[512,1024]{1,0:T(8,128)(2,1)S(1)}, u32[]{:S(2)}, u32[]{:S(2)}) %collective-permute-start.9) | collective-permute-done | bytes 1048608 | tf_op jit(solution)/shard_map/ppermute | solution.py:20
  144.5 3.0 %project.1 = bf16[8,8,16,128]{3,2,1,0:T(8,128)(2,1)} custom-call(s32[4]{0:T(128)} %pad_add_fusion.scalars, bf16[512,1024]{1,0:T(8,128)(2,1)} %bitcast.26, bf16[512,1024]{1,0:T(8,128)(2,1)} %copy-done.2, bf16[1024,128]{1,0:T(8,128)(2,1)} %weight.1), custom_call_target="tpu_custom_call" | custom-call | tf_op jit(solution)/shard_map/project/pallas_call | solution.py:273
  147.5 37.3 %all_to_all.11 = bf16[8,8,16,128]{3,2,1,0:T(8,128)(2,1)S(1)} all-to-all(bf16[8,8,16,128]{3,2,1,0:T(8,128)(2,1)} %project.1), channel_id=1, replica_groups=mesh['seq'=16,'tp'=8,'rep'=4] {'tp'}, dimensions={0} | all-to-all | bytes 524288 | tf_op jit(solution)/shard_map/all_to_all | solution.py:280
  (43 shorter events, 22.3 us)
Async XLA Ops:
  0.0 44.1 %copy-start.8 = (bf16[1,40,2,128]{3,2,1,0:T(2,128)(2,1)S(1)}, bf16[1,40,2,128]{3,2,1,0:T(2,128)(2,1)}, u32[]{:S(2)}) copy-start(bf16[1,40,2,128]{3,2,1,0:T(2,128)(2,1)} %param.13) | copy-start | bytes 61444
  0.0 15.5 %collective-permute-start = (bf16[40,1024]{1,0:T(8,128)(2,1)}, bf16[40,1024]{1,0:T(8,128)(2,1)S(1)}, u32[]{:S(2)}, u32[]{:S(2)}) collective-permute-start(bf16[40,1024]{1,0:T(8,128)(2,1)} %bitcast.29), channel_id=1, source_target_pairs={{0,256},{32,288},{64,320},{96,352},{128,384},{160,416},{192,448},{... | collective-permute-start | bytes 245768 | tf_op jit(solution)/shard_map/ppermute | solution.py:20
  16.4 10.3 %collective-permute-start.1 = (bf16[80,1024]{1,0:T(8,128)(2,1)S(1)}, bf16[80,1024]{1,0:T(8,128)(2,1)S(1)}, u32[]{:S(2)}, u32[]{:S(2)}) collective-permute-start(bf16[80,1024]{1,0:T(8,128)(2,1)S(1)} %pad_maximum_fusion.3), channel_id=1, source_target_pairs={{0,128},{32,160},{64,192},{96,224},{128,0},{160,32},{192,64},{224,... | collective-permute-start | bytes 491528 | tf_op jit(solution)/shard_map/ppermute | solution.py:20
  27.5 11.5 %collective-permute-start.2 = (bf16[160,1024]{1,0:T(8,128)(2,1)S(1)}, bf16[160,1024]{1,0:T(8,128)(2,1)S(1)}, u32[]{:S(2)}, u32[]{:S(2)}) collective-permute-start(bf16[160,1024]{1,0:T(8,128)(2,1)S(1)} %pad_maximum_fusion.1), channel_id=1, source_target_pairs={{0,64},{32,96},{64,0},{96,32},{128,192},{160,224},{192,128},{224,1... | collective-permute-start | bytes 983048 | tf_op jit(solution)/shard_map/ppermute | solution.py:20
  40.0 4.7 %copy-start.1 = (bf16[320,1024]{1,0:T(8,128)(2,1)}, bf16[320,1024]{1,0:T(8,128)(2,1)S(1)}, u32[]{:S(2)}) copy-start(bf16[320,1024]{1,0:T(8,128)(2,1)S(1)} %pad_maximum_fusion.near) | copy-start | bytes 1966084
  40.0 4.7 %collective-permute-start.3 = (bf16[320,1024]{1,0:T(8,128)(2,1)S(1)}, bf16[320,1024]{1,0:T(8,128)(2,1)S(1)}, u32[]{:S(2)}, u32[]{:S(2)}) collective-permute-start(bf16[320,1024]{1,0:T(8,128)(2,1)S(1)} %pad_maximum_fusion.near), channel_id=1, source_target_pairs={{0,32},{32,0},{64,96},{96,64},{128,160},{160,128},{192,224},{224,1... | collective-permute-start | bytes 1966088 | tf_op jit(solution)/shard_map/ppermute | solution.py:20
  44.7 0.9 copy-start.3
  58.7 3.8 %collective-permute-start.4 = (bf16[128,1152]{1,0:T(8,128)(2,1)}, bf16[128,1152]{1,0:T(8,128)(2,1)S(1)}, u32[]{:S(2)}, u32[]{:S(2)}) collective-permute-start(bf16[128,1152]{1,0:T(8,128)(2,1)} %get-tuple-element.10), channel_id=1, source_target_pairs={{0,32},{32,0},{64,96},{96,64},{128,160},{160,128},{192,224},{224,1... | collective-permute-start | bytes 884744 | tf_op jit(solution)/shard_map/ppermute | solution.py:20
  62.5 0.7 copy-start.4
  65.5 8.2 %collective-permute-start.5 = (bf16[64,1152]{1,0:T(8,128)(2,1)}, bf16[64,1152]{1,0:T(8,128)(2,1)S(1)}, u32[]{:S(2)}, u32[]{:S(2)}) collective-permute-start(bf16[64,1152]{1,0:T(8,128)(2,1)} %get-tuple-element.12), channel_id=1, source_target_pairs={{0,64},{32,96},{64,0},{96,32},{128,192},{160,224},{192,128},{224,1... | collective-permute-start | bytes 442376 | tf_op jit(solution)/shard_map/ppermute | solution.py:20
  73.7 0.7 copy-start.5
  76.3 11.3 %collective-permute-start.6 = (bf16[64,1152]{1,0:T(8,128)(2,1)}, bf16[64,1152]{1,0:T(8,128)(2,1)S(1)}, u32[]{:S(2)}, u32[]{:S(2)}) collective-permute-start(bf16[64,1152]{1,0:T(8,128)(2,1)} %join.5.refs_0_), channel_id=1, source_target_pairs={{0,128},{32,160},{64,192},{96,224},{128,0},{160,32},{192,64},{224,... | collective-permute-start | bytes 442376 | tf_op jit(solution)/shard_map/ppermute | solution.py:20
  87.5 0.6 copy-start.6
  90.2 16.6 %collective-permute-start.7 = (bf16[64,1152]{1,0:T(8,128)(2,1)}, bf16[64,1152]{1,0:T(8,128)(2,1)S(1)}, u32[]{:S(2)}, u32[]{:S(2)}) collective-permute-start(bf16[64,1152]{1,0:T(8,128)(2,1)} %join.6.refs_0_), channel_id=1, source_target_pairs={{0,256},{32,288},{64,320},{96,352},{128,384},{160,416},{192,448},{... | collective-permute-start | bytes 442376 | tf_op jit(solution)/shard_map/ppermute | solution.py:20
  106.8 0.6 copy-start.7
  109.4 9.9 %collective-permute-start.8 = (bf16[64,1024]{1,0:T(8,128)(2,1)}, bf16[64,1024]{1,0:T(8,128)(2,1)S(1)}, u32[]{:S(2)}, u32[]{:S(2)}) collective-permute-start(bf16[64,1024]{1,0:T(8,128)(2,1)} %join.7), channel_id=1, source_target_pairs={{0,64},{32,96},{64,0},{96,32},{128,192},{160,224},{192,128},{224,1... | collective-permute-start | bytes 393224 | tf_op jit(solution)/shard_map/ppermute | solution.py:20
  138.9 4.5 %copy-start = (bf16[4,128,1024]{2,1,0:T(8,128)(2,1)}, bf16[4,128,1024]{2,1,0:T(8,128)(2,1)S(1)}, u32[]{:S(2)}) copy-start(bf16[4,128,1024]{2,1,0:T(8,128)(2,1)S(1)} %all_to_all.10) | copy-start | bytes 3145732
  138.9 4.5 %collective-permute-start.9 = (bf16[512,1024]{1,0:T(8,128)(2,1)S(1)}, bf16[512,1024]{1,0:T(8,128)(2,1)S(1)}, u32[]{:S(2)}, u32[]{:S(2)}) collective-permute-start(bf16[512,1024]{1,0:T(8,128)(2,1)S(1)} %bitcast.25), channel_id=1, source_target_pairs={{0,32},{32,0},{64,96},{96,64},{128,160},{160,128},{192,224},{224,1... | collective-permute-start | bytes 3145736 | tf_op jit(solution)/shard_map/ppermute | solution.py:20
  143.5 1.0 copy-start.2

commit v2 on v1

v2 whole, which is shorter than its diff:
```python
import functools
import math

import jax
import jax.numpy as jnp
from jax import lax
from jax.experimental import pallas as pl
from jax.experimental.pallas import tpu as pltpu
from jax.sharding import PartitionSpec as P


HD = 128
LANES = 128
NEG = -1e30
BF = jnp.bfloat16
F32 = jnp.float32


def swap(x, axis, bit):
    size = lax.axis_size(axis)
    return lax.ppermute(x, axis, [(i, i ^ bit) for i in range(size)])


def dot(a, b):
    return lax.dot_general(a, b, (((1,), (0,)), ((), ())), preferred_element_type=F32)


def dot_t(a, b):
    return lax.dot_general(a, b, (((1,), (1,)), ((), ())), preferred_element_type=F32)


def split_stats(stat):
    hi = stat.astype(BF).astype(F32)
    rest = stat - hi
    mid = rest.astype(BF).astype(F32)
    low = rest - mid
    lane = lax.broadcasted_iota(jnp.int32, stat.shape, 1)
    out = jnp.where(lane < 8, hi, jnp.where(lane < 16, pltpu.roll(mid, 8, 1), pltpu.roll(low, 16, 1)))
    return jnp.where(lane < 24, out, 0.0).astype(BF)


def join_stats(packed):
    x = packed.astype(F32)
    return x + pltpu.roll(x, LANES - 8, 1) + pltpu.roll(x, LANES - 16, 1)


def heads_down(x, heads):
    return jnp.concatenate([x[:, h * HD : (h + 1) * HD] for h in range(heads)], axis=0)


def lanes_of(column, heads, rows):
    lane = lax.broadcasted_iota(jnp.int32, (rows, LANES), 1)
    out = jnp.zeros((rows, LANES), F32)
    for h in range(heads):
        out = jnp.where(lane == h, column[h * rows : (h + 1) * rows], out)
    return out


def one_hot(ids, width, offset=0):
    lane = lax.broadcasted_iota(jnp.int32, (ids.shape[0], width), 1)
    return jnp.where(ids - offset == lane, 1.0, 0.0).astype(BF)


def log_stats(top, mass, factor, heads, rows):
    return split_stats(lanes_of(top * factor + jnp.log2(mass), heads, rows))


def attend_kernel(heads, pairs, core, spos, dest, own_pos, gens, slots, new_kv, keys, other_keys, values, other_values, suf, out, suffix_out, sorted_rows):
    step = pl.program_id(0)
    width = heads * HD
    factor = HD**-0.5 * math.log2(math.e)

    def pick(ids):
        q = dot(one_hot(ids, slots.shape[0]), slots[...])
        return heads_down(q.astype(BF), heads)

    rows = spos.shape[0] // pairs
    for pair in range(pairs):
        ids = spos[pair * rows : (pair + 1) * rows]
        q = pick(ids)
        fresh = dot(one_hot(ids, new_kv.shape[0]), new_kv[...])
        fresh_k = jnp.concatenate([fresh[:, :HD]] * heads, axis=0)
        fresh_v = jnp.concatenate([fresh[:, HD:]] * heads, axis=0)
        mine = jnp.concatenate([ids] * heads, axis=0) < new_kv.shape[0]
        self_score = jnp.sum(q.astype(F32) * fresh_k, axis=1, keepdims=True)
        self_score = jnp.where(mine, self_score, NEG)
        near = dot_t(q, keys[pair])
        far = dot_t(q, other_keys[pair])
        peak = jnp.maximum(jnp.max(near, axis=1, keepdims=True), jnp.max(far, axis=1, keepdims=True))
        peak = jnp.maximum(peak, self_score)
        near = jnp.exp2((near - peak) * factor)
        far = jnp.exp2((far - peak) * factor)
        self_weight = jnp.exp2((self_score - peak) * factor)
        mass = jnp.sum(near, axis=1, keepdims=True) + jnp.sum(far, axis=1, keepdims=True) + self_weight
        mixed = dot(near.astype(BF), values[pair]) + dot(far.astype(BF), other_values[pair])
        mixed = mixed + self_weight.astype(BF).astype(F32) * fresh_v
        mixed = (mixed / mass).astype(BF)
        at = pl.ds(pl.multiple_of((step * pairs + pair) * rows, rows), rows)
        for h in range(heads):
            sorted_rows[at, h * HD : (h + 1) * HD] = mixed[h * rows : (h + 1) * rows]
        sorted_rows[at, width : width + LANES] = log_stats(peak, mass, factor, heads, rows)

    @pl.when(step == 0)
    def _():
        own = own_pos.shape[0] // 2
        tall = suf.shape[0] // 4
        for rel in range(2):
            qs = pick(own_pos[rel * own : (rel + 1) * own])
            base = rel * 2 * tall
            score = dot_t(qs, suf[base : base + tall])
            depth = tall // own
            row = lax.broadcasted_iota(jnp.int32, score.shape, 0) % own
            col = lax.broadcasted_iota(jnp.int32, score.shape, 1)
            length = jnp.concatenate([gens[rel * own : (rel + 1) * own]] * heads, axis=0)
            live = (col // depth == row) & (col % depth < length)
            score = jnp.where(live, score, NEG)
            top = jnp.max(score, axis=1, keepdims=True)
            w = jnp.where(live, jnp.exp2((score - top) * factor), 0.0)
            m = jnp.sum(w, axis=1, keepdims=True)
            o = (dot(w.astype(BF), suf[base + tall : base + 2 * tall]) / m).astype(BF)
            at = pl.ds(pl.multiple_of((core[0] ^ rel) * own, own), own)
            for h in range(heads):
                suffix_out[at, h * HD : (h + 1) * HD] = o[h * own : (h + 1) * own]
            suffix_out[at, width : width + LANES] = log_stats(top, m, factor, heads, own)

    @pl.when(step == pl.num_programs(0) - 1)
    def _():
        total = sorted_rows.shape[0]
        place = lax.broadcasted_iota(jnp.int32, (total, total), 0)
        to_dest = jnp.where(place == dest[...], 1.0, 0.0).astype(BF)
        placed = dot(to_dest, sorted_rows[...]).astype(BF)
        n = out.shape[1]
        for i in range(out.shape[0]):
            out[i] = placed[i * n : (i + 1) * n]


def join_kernel(heads, parts, suffix, out):
    width = heads * HD
    count = parts.shape[0]
    stats = [join_stats(parts[i, :, width : width + LANES]) for i in range(count)]
    stats.append(join_stats(suffix[:, width : width + LANES]))
    top = functools.reduce(jnp.maximum, stats)
    grown = [jnp.exp2(s - top) for s in stats]
    total = functools.reduce(jnp.add, grown)
    share = [e / total for e in grown]
    for h in range(heads):
        cut = slice(h * HD, (h + 1) * HD)
        o = suffix[:, cut].astype(F32) * share[count][:, h : h + 1]
        for i in range(count):
            o = o + parts[i, :, cut].astype(F32) * share[i][:, h : h + 1]
        o = o.astype(BF)
        for i in range(out.shape[0]):
            out[i, :, cut] = o


def project_kernel(spot, mine, partner, w0, w1, w2, w3, out):
    core, group = spot[0], spot[1]
    out[...] = jnp.zeros_like(out)
    depth = mine.shape[1]
    near = pl.ds(pl.multiple_of(core * depth, depth), depth)
    far = pl.ds(pl.multiple_of((1 - core) * depth, depth), depth)
    n = out.shape[1]
    for rel, w in enumerate((w0, w1, w2, w3)):
        y = (dot(mine[...], w[near, :]) + dot(partner[...], w[far, :])).astype(BF)
        for high in range(2):
            out[((group % 2) * 2 + high) * 4 + (group ^ rel)] = y[high * n : (high + 1) * n]


def plane_kernel(spot, parts, keep, send):
    sums = []
    for top in range(2):
        terms = [parts[y * 4 + top * 2 + g].astype(F32) for y in range(4) for g in range(2)]
        sums.append(functools.reduce(jnp.add, terms))
    upper = spot[2] == 1
    keep[...] = jnp.where(upper, sums[1], sums[0])
    send[...] = jnp.where(upper, sums[0], sums[1]).astype(BF)


VMEM = pl.BlockSpec(memory_space=pltpu.VMEM)
SMEM = pl.BlockSpec(memory_space=pltpu.SMEM)


def body(counts, prompt_of, queries, new_kv, prompt_keys, prompt_values, suffix_keys, suffix_values, gen_len, out_weight):
    me = lax.axis_index("seq")
    core, chip = me & 1, me >> 1
    group = lax.axis_index("rep")
    upper = lax.axis_index("tp") >> 2
    capacity, width = queries.shape[1:]
    heads = width // HD // 2
    half = heads * HD
    per_device = gen_len.shape[1]
    seq_count = lax.axis_size("seq")
    chips = seq_count // 2
    total = per_device * seq_count
    prompts, depth = prompt_keys.shape[1:3]
    block = total // prompts
    line = [[2 * i + c for i in range(chips)] for c in range(2)]

    halves = queries[0][:, :half], queries[0][:, half:]
    low = core == 0
    mine = jnp.where(low, halves[0], halves[1])
    theirs = jnp.where(low, halves[1], halves[0])
    slots = jnp.concatenate([mine, swap(theirs, "seq", 1)], axis=0)

    small = jnp.concatenate(
        [
            new_kv[0].reshape(capacity, 2 * HD),
            jnp.broadcast_to(gen_len[0].astype(BF)[:, None], (per_device, 2 * HD)),
        ],
        axis=0,
    )
    suffix = jnp.concatenate([suffix_keys[0].reshape(-1, HD), suffix_values[0].reshape(-1, HD)], axis=0)
    slots, small, suffix, keys, values, weight = lax.optimization_barrier(
        (slots, small, suffix, prompt_keys[0], prompt_values[0], out_weight)
    )
    for bit in (8, 4, 2):
        slots = jnp.concatenate([slots, swap(slots, "seq", bit)], axis=0)
    other_small = swap(small, "seq", 1)
    other_suffix = swap(suffix, "seq", 1)
    other_keys = swap(keys, "seq", 1)
    other_values = swap(values, "seq", 1)
    weights = [weight] + [swap(weight, "rep", bit) for bit in (1, 2, 3)]

    new_pairs = jnp.concatenate([small[:capacity], other_small[:capacity]], axis=0)
    gens = jnp.concatenate([small[capacity:, :1], other_small[capacity:, :1]], axis=0).astype(jnp.int32)
    suffixes = jnp.concatenate([suffix, other_suffix], axis=0)

    tally = counts[0]
    ends = jnp.cumsum(tally)
    row = jnp.arange(total, dtype=jnp.int32)
    past = ends[None, :] <= row[:, None]
    holder = jnp.sum(past.astype(jnp.int32), axis=1)
    offset = row - jnp.sum(jnp.where(past, tally[None, :], 0), axis=1)
    away = (holder >> 1) ^ chip
    slot = (((away >> 2) & 1) + ((away >> 1) & 1) * 2 + (away & 1) * 4) * (2 * capacity)
    slot = slot + ((holder & 1) ^ core) * capacity + offset
    prompt = prompt_of[0]
    before = (prompt[None, :] == prompt[:, None]) & (row[None, :] < row[:, None])
    rank = prompt * block + jnp.sum(before.astype(jnp.int32), axis=1)
    at_rank = rank[None, :] == row[:, None]
    slot_sorted = jnp.sum(jnp.where(at_rank, slot[None, :], 0), axis=1)
    dest_sorted = jnp.sum(jnp.where(at_rank, row[None, :], 0), axis=1)
    local = jnp.arange(2 * per_device, dtype=jnp.int32)
    local = (me ^ (local // per_device)) * per_device + local % per_device
    own_slot = jnp.sum(jnp.where(local[:, None] == row[None, :], slot[None, :], 0), axis=1)
    spot = jnp.stack([core, group, upper]).astype(jnp.int32)

    packed = half + LANES
    pairs = 2
    whole = lambda *shape: pl.BlockSpec(shape, lambda i, s: (0,) * len(shape))
    cache = pl.BlockSpec((pairs, depth, HD), lambda i, s: (i, 0, 0))
    parts, own_part = pl.pallas_call(
        functools.partial(attend_kernel, heads, pairs),
        out_shape=[
            jax.ShapeDtypeStruct((chips, total // chips, packed), BF),
            jax.ShapeDtypeStruct((2 * per_device, packed), BF),
        ],
        grid_spec=pltpu.PrefetchScalarGridSpec(
            num_scalar_prefetch=1,
            grid=(prompts // pairs,),
            in_specs=[
                pl.BlockSpec((block * pairs, 1), lambda i, s: (i, 0)),
                whole(1, total),
                whole(2 * per_device, 1),
                whole(2 * per_device, 1),
                whole(*slots.shape),
                whole(*new_pairs.shape),
                cache,
                cache,
                cache,
                cache,
                whole(*suffixes.shape),
            ],
            out_specs=[whole(chips, total // chips, packed), whole(2 * per_device, packed)],
            scratch_shapes=[pltpu.VMEM((total, packed), BF)],
        ),
        compiler_params=pltpu.CompilerParams(vmem_limit_bytes=20 << 20),
        name="attend",
    )(
        spot,
        slot_sorted[:, None],
        dest_sorted[None, :],
        own_slot[:, None],
        gens,
        slots,
        new_pairs,
        keys,
        other_keys,
        values,
        other_values,
        suffixes,
    )
    parts = lax.all_to_all(parts, "seq", 0, 0, axis_index_groups=line, tiled=True)
    spread = pl.pallas_call(
        functools.partial(join_kernel, heads),
        out_shape=jax.ShapeDtypeStruct((chips, 2 * per_device, half), BF),
        in_specs=[VMEM] * 2,
        out_specs=VMEM,
        compiler_params=pltpu.CompilerParams(vmem_limit_bytes=8 << 20),
        name="join",
    )(parts, own_part)
    attended = lax.all_to_all(spread, "seq", 0, 0, axis_index_groups=line, tiled=True).reshape(total, half)
    partner = swap(attended, "seq", 1)
    columns = out_weight.shape[1]
    plane = [[(z * 4 + y) * 4 + x for y in range(4) for x in range(4)] for z in range(2)]
    products = pl.pallas_call(
        project_kernel,
        out_shape=jax.ShapeDtypeStruct((16, total // 2, columns), BF),
        in_specs=[SMEM] + [VMEM] * 6,
        out_specs=VMEM,
        compiler_params=pltpu.CompilerParams(vmem_limit_bytes=8 << 20),
        name="project",
    )(spot, attended, partner, *weights)
    products = lax.all_to_all(products, ("tp", "rep"), 0, 0, axis_index_groups=plane, tiled=True)
    keep, send = pl.pallas_call(
        plane_kernel,
        out_shape=[
            jax.ShapeDtypeStruct((total // 2, columns), F32),
            jax.ShapeDtypeStruct((total // 2, columns), BF),
        ],
        in_specs=[SMEM, VMEM],
        out_specs=[VMEM] * 2,
        compiler_params=pltpu.CompilerParams(vmem_limit_bytes=8 << 20),
        name="plane",
    )(spot, products)
    return (keep + swap(send, "tp", 4).astype(F32)).astype(BF)


def solution(mesh):
    in_specs = (
        P("rep", None),
        P("rep", None),
        P("rep", "seq", "tp"),
        P("rep", "seq", None, "tp"),
        P("rep", None, "seq", "tp"),
        P("rep", None, "seq", "tp"),
        P("rep", "seq", None, "tp"),
        P("rep", "seq", None, "tp"),
        P("rep", "seq"),
        P("tp", ("seq", "rep")),
    )
    out_specs = P("tp", ("seq", "rep"))
    return jax.shard_map(body, mesh=mesh, in_specs=in_specs, out_specs=out_specs, check_vma=False)
```

time: 186 us -> 155 us (0.83)
  the two profiles are of different devices: /device:TPU:32 before, /device:TPU:6 now
where the time goes in v2:
time: 155 us; the launch traced here: 152 us
  starting transfers between devices  48.7 us (31%)
  blocking collectives  43.8 us (28%)
  waiting for transfers between devices  36.2 us (23%)
  Pallas kernels  13.6 us (9%)
  other arithmetic  7.4 us (5%)
  local copies, waits for them, and re-layouts  1.8 us (1%)
    ppermute x13, starting transfers between devices, swap(): return lax.ppermute(x, axis, [(i, i ^ bit) for i in range(size)])  44.2 us
    ppermute x13, waiting for transfers between devices, swap(): return lax.ppermute(x, axis, [(i, i ^ bit) for i in range(size)])  28.8 us
    all_to_all x1, blocking collectives, body(): lax.all_to_all(parts, 'seq', 0, 0, axis_index_groups=line, tiled=True)  27.3 us
    all_to_all x1, blocking collectives, body(): lax.all_to_all(products, ('tp', 'rep'), 0, 0, axis_index_groups=plane, ti...  16.4 us
    pallas_call x1, Pallas kernels, body(): pl.pallas_call(functools.partial(attend_kernel, heads, pairs), out_shape=...  10.6 us
    all_to_all x1, waiting for transfers between devices, body(): lax.all_to_all(spread, 'seq', 0, 0, axis_index_groups=line, tiled=True)  7.34 us
    all_to_all x1, starting transfers between devices, body(): lax.all_to_all(spread, 'seq', 0, 0, axis_index_groups=line, tiled=True)  4.45 us
  transfers between devices with their start and end apart: 14, of which 6 were waited for; matrix products, arithmetic and copies ran while one was open for 5% of the time, Pallas kernels for 0%

profile of v2, /device:TPU:6, one launch (start us, length us, event | category | flops | bytes accessed | tf_op | source)
XLA Modules:
  0.0 151.8 jit_solution(15535854082551805917)
XLA Ops:
  0.8 1.9 %collective-permute-start = (bf16[40,512]{1,0:T(8,128)(2,1)S(1)}, bf16[40,512]{1,0:T(8,128)(2,1)S(1)}, u32[]{:S(2)}, u32[]{:S(2)}) collective-permute-start(bf16[40,512]{1,0:T(8,128)(2,1)S(1)} %get-tuple-element.30), channel_id=1, source_target_pairs={{0,32},{32,0},{64,96},{96,64},{128,160},{160,128},{192,224},{224,1... | collective-permute-start | bytes 122888 | tf_op jit(solution)/shard_map/ppermute | solution.py:21
  6.3 2.4 %collective-permute-start.5 = (bf16[8,1024,128]{2,1,0:T(8,128)(2,1)}, bf16[8,1024,128]{2,1,0:T(8,128)(2,1)S(1)}, u32[]{:S(2)}, u32[]{:S(2)}) collective-permute-start(bf16[8,1024,128]{2,1,0:T(8,128)(2,1)} %bitcast.24), channel_id=1, source_target_pairs={{0,32},{32,0},{64,96},{96,64},{128,160},{160,128},{192,224},{224,1... | collective-permute-start | bytes 6291464 | tf_op jit(solution)/shard_map/ppermute | solution.py:21
  8.7 1.9 %collective-permute-start.6 = (bf16[8,1024,128]{2,1,0:T(8,128)(2,1)}, bf16[8,1024,128]{2,1,0:T(8,128)(2,1)}, u32[]{:S(2)}, u32[]{:S(2)}) collective-permute-start(bf16[8,1024,128]{2,1,0:T(8,128)(2,1)} %bitcast.26), channel_id=1, source_target_pairs={{0,32},{32,0},{64,96},{96,64},{128,160},{160,128},{192,224},{224,1... | collective-permute-start | bytes 6291464 | tf_op jit(solution)/shard_map/ppermute | solution.py:21
  13.3 9.1 %collective-permute-start.2 = (bf16[80,512]{1,0:T(8,128)(2,1)S(1)}, bf16[80,512]{1,0:T(8,128)(2,1)S(1)}, u32[]{:S(2)}, u32[]{:S(2)}) collective-permute-start(bf16[80,512]{1,0:T(8,128)(2,1)S(1)} %pad_maximum_fusion.5), channel_id=1, source_target_pairs={{0,256},{32,288},{64,320},{96,352},{128,384},{160,416},{192,448},{... | collective-permute-start | bytes 245768 | tf_op jit(solution)/shard_map/ppermute | solution.py:21
  22.5 2.1 %collective-permute-start.1 = (bf16[56,256]{1,0:T(8,128)(2,1)S(1)}, bf16[56,256]{1,0:T(8,128)(2,1)S(1)}, u32[]{:S(2)}, u32[]{:S(2)}) collective-permute-start(bf16[56,256]{1,0:T(8,128)(2,1)S(1)} %pad_maximum_fusion.7), channel_id=1, source_target_pairs={{0,32},{32,0},{64,96},{96,64},{128,160},{160,128},{192,224},{224,1... | collective-permute-start | bytes 86024 | tf_op jit(solution)/shard_map/ppermute | solution.py:21
  24.6 2.2 %collective-permute-start.7 = (bf16[2048,128]{1,0:T(8,128)(2,1)S(1)}, bf16[2048,128]{1,0:T(8,128)(2,1)}, u32[]{:S(2)}, u32[]{:S(2)}) collective-permute-start(bf16[2048,128]{1,0:T(8,128)(2,1)S(1)} %pad_maximum_fusion.2), channel_id=1, source_target_pairs={{0,32},{32,0},{64,96},{96,64},{128,160},{160,128},{192,224},{224,1... | collective-permute-start | bytes 1572872 | tf_op jit(solution)/shard_map/ppermute | solution.py:21
  27.1 3.7 %collective-permute-done.2 = bf16[80,512]{1,0:T(8,128)(2,1)S(1)} collective-permute-done((bf16[80,512]{1,0:T(8,128)(2,1)S(1)}, bf16[80,512]{1,0:T(8,128)(2,1)S(1)}, u32[]{:S(2)}, u32[]{:S(2)}) %collective-permute-start.2) | collective-permute-done | bytes 81952 | tf_op jit(solution)/shard_map/ppermute | solution.py:21
  30.8 1.9 %collective-permute-start.3 = (bf16[160,512]{1,0:T(8,128)(2,1)S(1)}, bf16[160,512]{1,0:T(8,128)(2,1)S(1)}, u32[]{:S(2)}, u32[]{:S(2)}) collective-permute-start(bf16[160,512]{1,0:T(8,128)(2,1)S(1)} %pad_maximum_fusion.4), channel_id=1, source_target_pairs={{0,128},{32,160},{64,192},{96,224},{128,0},{160,32},{192,64},{224,... | collective-permute-start | bytes 491528 | tf_op jit(solution)/shard_map/ppermute | solution.py:21
  32.8 10.3 %collective-permute-done.3 = bf16[160,512]{1,0:T(8,128)(2,1)S(1)} collective-permute-done((bf16[160,512]{1,0:T(8,128)(2,1)S(1)}, bf16[160,512]{1,0:T(8,128)(2,1)S(1)}, u32[]{:S(2)}, u32[]{:S(2)}) %collective-permute-start.3) | collective-permute-done | bytes 163872 | tf_op jit(solution)/shard_map/ppermute | solution.py:21
  43.2 1.9 %collective-permute-start.4 = (bf16[320,512]{1,0:T(8,128)(2,1)S(1)}, bf16[320,512]{1,0:T(8,128)(2,1)S(1)}, u32[]{:S(2)}, u32[]{:S(2)}) collective-permute-start(bf16[320,512]{1,0:T(8,128)(2,1)S(1)} %pad_maximum_fusion.3), channel_id=1, source_target_pairs={{0,64},{32,96},{64,0},{96,32},{128,192},{160,224},{192,128},{224,1... | collective-permute-start | bytes 983048 | tf_op jit(solution)/shard_map/ppermute | solution.py:21
  46.2 8.4 %collective-permute-done.4 = bf16[320,512]{1,0:T(8,128)(2,1)S(1)} collective-permute-done((bf16[320,512]{1,0:T(8,128)(2,1)S(1)}, bf16[320,512]{1,0:T(8,128)(2,1)S(1)}, u32[]{:S(2)}, u32[]{:S(2)}) %collective-permute-start.4) | collective-permute-done | bytes 327712 | tf_op jit(solution)/shard_map/ppermute | solution.py:21
  54.8 10.6 %attend.1 = (bf16[8,32,640]{2,1,0:T(8,128)(2,1)S(1)}, bf16[32,640]{1,0:T(8,128)(2,1)S(1)}) custom-call(s32[3]{0:T(128)S(1)} %pad_add_fusion.core.spot, s32[256,1]{1,0:T(8,128)S(1)} %copy.23.spos, s32[1,256]{1,0:T(1,128)S(1)} %bitcast.30, s32[32,1]{1,0:T(8,128)S(1)} %copy.24.own_pos, s32[32,1]{1,0:T(8,128)S(1)} %maximum_convert_fusion.gens, ...), custom_call_target="tpu_custom_call" | custom-call | tf_op jit(solution)/shard_map/attend/pallas_call | solution.py:252
  65.4 27.3 %all_to_all.15.parts = bf16[8,32,640]{2,1,0:T(8,128)(2,1)S(1)} all-to-all(bf16[8,32,640]{2,1,0:T(8,128)(2,1)S(1)} %get-tuple-element.20), channel_id=1, replica_groups={{0,64,128,192,256,320,384,448},{32,96,160,224,288,352,416,480},{1,65,12..., dimensions={0} | all-to-all | bytes 655360 | tf_op jit(solution)/shard_map/all_to_all | solution.py:293
  93.8 4.5 %all-to-all-start.1 = ((bf16[8,32,512]{2,1,0:T(8,128)(2,1)}), bf16[8,32,512]{2,1,0:T(8,128)(2,1)S(1)}, u32[]{:S(2)}, u32[]{:S(2)}) async-start(bf16[8,32,512]{2,1,0:T(8,128)(2,1)} %join.1), calls=%async_computation.1 | async-start | bytes 524288 | tf_op jit(solution)/shard_map/all_to_all | solution.py:302
  98.3 3.3 %collective-permute-start.10 = (bf16[1024,128]{1,0:T(8,128)(2,1)S(1)}, bf16[1024,128]{1,0:T(8,128)(2,1)S(1)}, u32[]{:S(2)}, u32[]{:S(2)}) collective-permute-start(bf16[1024,128]{1,0:T(8,128)(2,1)S(1)} %copy-done.2), channel_id=1, source_target_pairs={{0,2},{1,3},{2,0},{3,1},{4,6},{5,7},{6,4},{7,5},{8,10},{9,11},{10,... | collective-permute-start | bytes 786440 | tf_op jit(solution)/shard_map/ppermute | solution.py:21
  101.6 4.0 %collective-permute-start.11 = (bf16[1024,128]{1,0:T(8,128)(2,1)S(1)}, bf16[1024,128]{1,0:T(8,128)(2,1)S(1)}, u32[]{:S(2)}, u32[]{:S(2)}) collective-permute-start(bf16[1024,128]{1,0:T(8,128)(2,1)S(1)} %copy-done.2), channel_id=1, source_target_pairs={{0,3},{1,2},{2,1},{3,0},{4,7},{5,6},{6,5},{7,4},{8,11},{9,10},{10,... | collective-permute-start | bytes 786440 | tf_op jit(solution)/shard_map/ppermute | solution.py:21
  105.6 1.9 %collective-permute-start.9 = (bf16[1024,128]{1,0:T(8,128)(2,1)S(1)}, bf16[1024,128]{1,0:T(8,128)(2,1)S(1)}, u32[]{:S(2)}, u32[]{:S(2)}) collective-permute-start(bf16[1024,128]{1,0:T(8,128)(2,1)S(1)} %copy-done.2), channel_id=1, source_target_pairs={{0,1},{1,0},{2,3},{3,2},{4,5},{5,4},{6,7},{7,6},{8,9},{9,8},{10,11... | collective-permute-start | bytes 786440 | tf_op jit(solution)/shard_map/ppermute | solution.py:21
  107.5 7.3 %all-to-all-done.1 = bf16[8,32,512]{2,1,0:T(8,128)(2,1)S(1)} async-done(((bf16[8,32,512]{2,1,0:T(8,128)(2,1)}), bf16[8,32,512]{2,1,0:T(8,128)(2,1)S(1)}, u32[]{:S(2)}, u32[]{:S(2)}) %all-to-all-start.1) | async-done | bytes 262176 | tf_op jit(solution)/shard_map/all_to_all | solution.py:302
  114.9 1.9 %collective-permute-start.8 = (bf16[256,512]{1,0:T(8,128)(2,1)S(1)}, bf16[256,512]{1,0:T(8,128)(2,1)S(1)}, u32[]{:S(2)}, u32[]{:S(2)}) collective-permute-start(bf16[256,512]{1,0:T(8,128)(2,1)S(1)} %bitcast.28), channel_id=1, source_target_pairs={{0,32},{32,0},{64,96},{96,64},{128,160},{160,128},{192,224},{224,1... | collective-permute-start | bytes 786440 | tf_op jit(solution)/shard_map/ppermute | solution.py:21
  116.8 1.5 collective-permute-done.8.partner
  118.3 1.3 project.1
  119.6 16.4 %all_to_all.16.parts = bf16[16,128,128]{2,1,0:T(8,128)(2,1)S(1)} all-to-all(bf16[16,128,128]{2,1,0:T(8,128)(2,1)S(1)} %project.1), channel_id=1, replica_groups={{0,1,2,3,4,5,6,7,8,9,10,11,12,13,14,15},{16,17,18,19,20,21,22,23,24,25,..., dimensions={0} | all-to-all | bytes 1048576 | tf_op jit(solution)/shard_map/all_to_all | solution.py:314
  136.6 9.6 %collective-permute-start.12 = (bf16[128,128]{1,0:T(8,128)(2,1)S(1)}, bf16[128,128]{1,0:T(8,128)(2,1)S(1)}, u32[]{:S(2)}, u32[]{:S(2)}) collective-permute-start(bf16[128,128]{1,0:T(8,128)(2,1)S(1)} %get-tuple-element.24), channel_id=1, source_target_pairs={{0,16},{4,20},{8,24},{12,28},{16,0},{20,4},{24,8},{28,12},{1,17},{... | collective-permute-start | bytes 98312 | tf_op jit(solution)/shard_map/ppermute | solution.py:21
  146.2 4.9 %collective-permute-done.12 = bf16[128,128]{1,0:T(8,128)(2,1)S(1)} collective-permute-done((bf16[128,128]{1,0:T(8,128)(2,1)S(1)}, bf16[128,128]{1,0:T(8,128)(2,1)S(1)}, u32[]{:S(2)}, u32[]{:S(2)}) %collective-permute-start.12) | collective-permute-done | bytes 32800 | tf_op jit(solution)/shard_map/ppermute | solution.py:21
  (47 shorter events, 10.9 us)
Async XLA Ops:
  0.8 5.4 %collective-permute-start = (bf16[40,512]{1,0:T(8,128)(2,1)S(1)}, bf16[40,512]{1,0:T(8,128)(2,1)S(1)}, u32[]{:S(2)}, u32[]{:S(2)}) collective-permute-start(bf16[40,512]{1,0:T(8,128)(2,1)S(1)} %get-tuple-element.30), channel_id=1, source_target_pairs={{0,32},{32,0},{64,96},{96,64},{128,160},{160,128},{192,224},{224,1... | collective-permute-start | bytes 122888 | tf_op jit(solution)/shard_map/ppermute | solution.py:21
  6.3 48.4 %collective-permute-start.5 = (bf16[8,1024,128]{2,1,0:T(8,128)(2,1)}, bf16[8,1024,128]{2,1,0:T(8,128)(2,1)S(1)}, u32[]{:S(2)}, u32[]{:S(2)}) collective-permute-start(bf16[8,1024,128]{2,1,0:T(8,128)(2,1)} %bitcast.24), channel_id=1, source_target_pairs={{0,32},{32,0},{64,96},{96,64},{128,160},{160,128},{192,224},{224,1... | collective-permute-start | bytes 6291464 | tf_op jit(solution)/shard_map/ppermute | solution.py:21
  8.7 46.0 %collective-permute-start.6 = (bf16[8,1024,128]{2,1,0:T(8,128)(2,1)}, bf16[8,1024,128]{2,1,0:T(8,128)(2,1)}, u32[]{:S(2)}, u32[]{:S(2)}) collective-permute-start(bf16[8,1024,128]{2,1,0:T(8,128)(2,1)} %bitcast.26), channel_id=1, source_target_pairs={{0,32},{32,0},{64,96},{96,64},{128,160},{160,128},{192,224},{224,1... | collective-permute-start | bytes 6291464 | tf_op jit(solution)/shard_map/ppermute | solution.py:21
  13.3 17.5 %collective-permute-start.2 = (bf16[80,512]{1,0:T(8,128)(2,1)S(1)}, bf16[80,512]{1,0:T(8,128)(2,1)S(1)}, u32[]{:S(2)}, u32[]{:S(2)}) collective-permute-start(bf16[80,512]{1,0:T(8,128)(2,1)S(1)} %pad_maximum_fusion.5), channel_id=1, source_target_pairs={{0,256},{32,288},{64,320},{96,352},{128,384},{160,416},{192,448},{... | collective-permute-start | bytes 245768 | tf_op jit(solution)/shard_map/ppermute | solution.py:21
  22.5 4.7 %collective-permute-start.1 = (bf16[56,256]{1,0:T(8,128)(2,1)S(1)}, bf16[56,256]{1,0:T(8,128)(2,1)S(1)}, u32[]{:S(2)}, u32[]{:S(2)}) collective-permute-start(bf16[56,256]{1,0:T(8,128)(2,1)S(1)} %pad_maximum_fusion.7), channel_id=1, source_target_pairs={{0,32},{32,0},{64,96},{96,64},{128,160},{160,128},{192,224},{224,1... | collective-permute-start | bytes 86024 | tf_op jit(solution)/shard_map/ppermute | solution.py:21
  24.6 20.5 %collective-permute-start.7 = (bf16[2048,128]{1,0:T(8,128)(2,1)S(1)}, bf16[2048,128]{1,0:T(8,128)(2,1)}, u32[]{:S(2)}, u32[]{:S(2)}) collective-permute-start(bf16[2048,128]{1,0:T(8,128)(2,1)S(1)} %pad_maximum_fusion.2), channel_id=1, source_target_pairs={{0,32},{32,0},{64,96},{96,64},{128,160},{160,128},{192,224},{224,1... | collective-permute-start | bytes 1572872 | tf_op jit(solution)/shard_map/ppermute | solution.py:21
  30.8 12.3 %collective-permute-start.3 = (bf16[160,512]{1,0:T(8,128)(2,1)S(1)}, bf16[160,512]{1,0:T(8,128)(2,1)S(1)}, u32[]{:S(2)}, u32[]{:S(2)}) collective-permute-start(bf16[160,512]{1,0:T(8,128)(2,1)S(1)} %pad_maximum_fusion.4), channel_id=1, source_target_pairs={{0,128},{32,160},{64,192},{96,224},{128,0},{160,32},{192,64},{224,... | collective-permute-start | bytes 491528 | tf_op jit(solution)/shard_map/ppermute | solution.py:21
  32.8 22.0 %copy-start.1 = (bf16[1,8,1024,128]{3,2,1,0:T(8,128)(2,1)S(1)}, bf16[1,8,1024,128]{3,2,1,0:T(8,128)(2,1)}, u32[]{:S(2)}) copy-start(bf16[1,8,1024,128]{3,2,1,0:T(8,128)(2,1)} %param.15) | copy-start | bytes 6291460
  32.8 22.0 %copy-start = (bf16[1,8,1024,128]{3,2,1,0:T(8,128)(2,1)S(1)}, bf16[1,8,1024,128]{3,2,1,0:T(8,128)(2,1)}, u32[]{:S(2)}) copy-start(bf16[1,8,1024,128]{3,2,1,0:T(8,128)(2,1)} %param.14) | copy-start | bytes 6291460
  43.2 11.5 %collective-permute-start.4 = (bf16[320,512]{1,0:T(8,128)(2,1)S(1)}, bf16[320,512]{1,0:T(8,128)(2,1)S(1)}, u32[]{:S(2)}, u32[]{:S(2)}) collective-permute-start(bf16[320,512]{1,0:T(8,128)(2,1)S(1)} %pad_maximum_fusion.3), channel_id=1, source_target_pairs={{0,64},{32,96},{64,0},{96,32},{128,192},{160,224},{192,128},{224,1... | collective-permute-start | bytes 983048 | tf_op jit(solution)/shard_map/ppermute | solution.py:21
  54.8 43.5 %copy-start.2 = (bf16[1024,128]{1,0:T(8,128)(2,1)S(1)}, bf16[1024,128]{1,0:T(8,128)(2,1)}, u32[]{:S(2)}) copy-start(bf16[1024,128]{1,0:T(8,128)(2,1)} %w0) | copy-start | bytes 786436
  93.8 21.1 %all-to-all-start.1 = ((bf16[8,32,512]{2,1,0:T(8,128)(2,1)}), bf16[8,32,512]{2,1,0:T(8,128)(2,1)S(1)}, u32[]{:S(2)}, u32[]{:S(2)}) async-start(bf16[8,32,512]{2,1,0:T(8,128)(2,1)} %join.1), calls=%async_computation.1 | async-start | bytes 524288 | tf_op jit(solution)/shard_map/all_to_all | solution.py:302
  98.3 18.5 %collective-permute-start.10 = (bf16[1024,128]{1,0:T(8,128)(2,1)S(1)}, bf16[1024,128]{1,0:T(8,128)(2,1)S(1)}, u32[]{:S(2)}, u32[]{:S(2)}) collective-permute-start(bf16[1024,128]{1,0:T(8,128)(2,1)S(1)} %copy-done.2), channel_id=1, source_target_pairs={{0,2},{1,3},{2,0},{3,1},{4,6},{5,7},{6,4},{7,5},{8,10},{9,11},{10,... | collective-permute-start | bytes 786440 | tf_op jit(solution)/shard_map/ppermute | solution.py:21
  101.6 15.2 %collective-permute-start.11 = (bf16[1024,128]{1,0:T(8,128)(2,1)S(1)}, bf16[1024,128]{1,0:T(8,128)(2,1)S(1)}, u32[]{:S(2)}, u32[]{:S(2)}) collective-permute-start(bf16[1024,128]{1,0:T(8,128)(2,1)S(1)} %copy-done.2), channel_id=1, source_target_pairs={{0,3},{1,2},{2,1},{3,0},{4,7},{5,6},{6,5},{7,4},{8,11},{9,10},{10,... | collective-permute-start | bytes 786440 | tf_op jit(solution)/shard_map/ppermute | solution.py:21
  105.6 11.2 %collective-permute-start.9 = (bf16[1024,128]{1,0:T(8,128)(2,1)S(1)}, bf16[1024,128]{1,0:T(8,128)(2,1)S(1)}, u32[]{:S(2)}, u32[]{:S(2)}) collective-permute-start(bf16[1024,128]{1,0:T(8,128)(2,1)S(1)} %copy-done.2), channel_id=1, source_target_pairs={{0,1},{1,0},{2,3},{3,2},{4,5},{5,4},{6,7},{7,6},{8,9},{9,8},{10,11... | collective-permute-start | bytes 786440 | tf_op jit(solution)/shard_map/ppermute | solution.py:21
  114.9 3.4 %collective-permute-start.8 = (bf16[256,512]{1,0:T(8,128)(2,1)S(1)}, bf16[256,512]{1,0:T(8,128)(2,1)S(1)}, u32[]{:S(2)}, u32[]{:S(2)}) collective-permute-start(bf16[256,512]{1,0:T(8,128)(2,1)S(1)} %bitcast.28), channel_id=1, source_target_pairs={{0,32},{32,0},{64,96},{96,64},{128,160},{160,128},{192,224},{224,1... | collective-permute-start | bytes 786440 | tf_op jit(solution)/shard_map/ppermute | solution.py:21
  136.6 14.5 %collective-permute-start.12 = (bf16[128,128]{1,0:T(8,128)(2,1)S(1)}, bf16[128,128]{1,0:T(8,128)(2,1)S(1)}, u32[]{:S(2)}, u32[]{:S(2)}) collective-permute-start(bf16[128,128]{1,0:T(8,128)(2,1)S(1)} %get-tuple-element.24), channel_id=1, source_target_pairs={{0,16},{4,20},{8,24},{12,28},{16,0},{20,4},{24,8},{28,12},{1,17},{... | collective-permute-start | bytes 98312 | tf_op jit(solution)/shard_map/ppermute | solution.py:21

commit v3 on v2

v3 whole, which is shorter than its diff:
```python
import functools
import math

import jax
import jax.numpy as jnp
from jax import lax
from jax.experimental import pallas as pl
from jax.experimental.pallas import tpu as pltpu
from jax.sharding import PartitionSpec as P


HD = 128
LANES = 128
NEG = -1e30
BF = jnp.bfloat16
F32 = jnp.float32


def swap(x, axis, bit):
    size = lax.axis_size(axis)
    return lax.ppermute(x, axis, [(i, i ^ bit) for i in range(size)])


def dot(a, b):
    return lax.dot_general(a, b, (((1,), (0,)), ((), ())), preferred_element_type=F32)


def dot_t(a, b):
    return lax.dot_general(a, b, (((1,), (1,)), ((), ())), preferred_element_type=F32)


def split_stats(stat):
    hi = stat.astype(BF).astype(F32)
    rest = stat - hi
    mid = rest.astype(BF).astype(F32)
    low = rest - mid
    lane = lax.broadcasted_iota(jnp.int32, stat.shape, 1)
    out = jnp.where(lane < 8, hi, jnp.where(lane < 16, pltpu.roll(mid, 8, 1), pltpu.roll(low, 16, 1)))
    return jnp.where(lane < 24, out, 0.0).astype(BF)


def join_stats(packed):
    x = packed.astype(F32)
    return x + pltpu.roll(x, LANES - 8, 1) + pltpu.roll(x, LANES - 16, 1)


def heads_down(x, heads):
    return jnp.concatenate([x[:, h * HD : (h + 1) * HD] for h in range(heads)], axis=0)


def lanes_of(column, heads, rows):
    lane = lax.broadcasted_iota(jnp.int32, (rows, LANES), 1)
    out = jnp.zeros((rows, LANES), F32)
    for h in range(heads):
        out = jnp.where(lane == h, column[h * rows : (h + 1) * rows], out)
    return out


def one_hot(ids, width, offset=0):
    lane = lax.broadcasted_iota(jnp.int32, (ids.shape[0], width), 1)
    return jnp.where(ids - offset == lane, 1.0, 0.0).astype(BF)


def log_stats(top, mass, factor, heads, rows):
    return split_stats(lanes_of(top * factor + jnp.log2(mass), heads, rows))


def order_kernel(block, slot_rows, spot, counts, prompt, slot_of, rank_of, own_slot):
    core, chip = spot[0], spot[3]
    total = prompt.shape[1]
    capacity = slot_rows
    row = lax.broadcasted_iota(jnp.int32, (1, total), 1)
    end = jnp.int32(0)
    holder = jnp.zeros((1, total), jnp.int32)
    offset = row
    for s in range(counts.shape[1]):
        count = counts[0, s]
        end = end + count
        past = row >= end
        holder = holder + jnp.where(past, 1, 0)
        offset = offset - jnp.where(past, count, 0)
    away = (holder >> 1) ^ chip
    place = ((holder & 1) ^ core) + ((away >> 2) & 1) * 2 + ((away >> 1) & 1) * 4 + (away & 1) * 8
    slot = place * capacity + offset
    lane = lax.broadcasted_iota(jnp.int32, (total, total), 1)
    sub = lax.broadcasted_iota(jnp.int32, (total, total), 0)
    across = jnp.broadcast_to(prompt[...], (total, total))
    down = jnp.sum(jnp.where(lane == sub, across, 0), axis=1, keepdims=True)
    same = across == down
    rank_of[...] = down * block + jnp.sum(jnp.where(same & (lane < sub), 1, 0), axis=1, keepdims=True)
    rank = prompt[...] * block + jnp.sum(jnp.where(same & (sub < lane), 1, 0), axis=0, keepdims=True)
    slot_of[...] = jnp.sum(jnp.where(rank == sub, slot, 0), axis=1, keepdims=True)
    n = own_slot.shape[0]
    local = lax.broadcasted_iota(jnp.int32, (n, total), 0)
    own = n // 2
    local = ((2 * chip + core) ^ (local // own)) * own + local % own
    own_slot[...] = jnp.sum(jnp.where(local == lane[:n], slot, 0), axis=1, keepdims=True)


def attend_kernel(heads, spot, slot_of, rank_of, own_slot, near, far, small, other_small, keys, other_keys, values, other_values, suf, other_suf, out, suffix_out, sorted_rows, queries, fresh_rows):
    core = spot[0]
    width = heads * HD
    factor = HD**-0.5 * math.log2(math.e)
    prompts = keys.shape[0]
    total = slot_of.shape[0]
    rows = total // prompts
    half = near.shape[0]
    own = own_slot.shape[0] // 2
    capacity = small.shape[0] - own

    def pick(ids):
        return (dot(one_hot(ids, half), near[...]) + dot(one_hot(ids, half, half), far[...])).astype(BF)

    ids = slot_of[...]
    q = pick(jnp.concatenate([ids, own_slot[...]], axis=0))
    own_q = q[total:]
    for p in range(prompts):
        for h in range(heads):
            queries[p, h * rows : (h + 1) * rows] = q[p * rows : (p + 1) * rows, h * HD : (h + 1) * HD]
    fresh_rows[...] = dot(one_hot(ids, capacity), small[:capacity]) + dot(
        one_hot(ids, capacity, capacity), other_small[:capacity]
    )

    def score(p):
        q = queries[p]
        return dot_t(q, keys[p]), dot_t(q, other_keys[p])

    def finish(p, scores):
        a, b = scores
        fresh = fresh_rows[p * rows : (p + 1) * rows]
        fresh_k = jnp.concatenate([fresh[:, :HD]] * heads, axis=0)
        fresh_v = jnp.concatenate([fresh[:, HD:]] * heads, axis=0)
        mine = jnp.concatenate([slot_of[p * rows : (p + 1) * rows]] * heads, axis=0) < 2 * capacity
        self_score = jnp.sum(queries[p].astype(F32) * fresh_k, axis=1, keepdims=True)
        self_score = jnp.where(mine, self_score, NEG)
        peak = jnp.max(jnp.maximum(a, b), axis=1, keepdims=True)
        peak = jnp.maximum(peak, self_score)
        a = jnp.exp2((a - peak) * factor)
        b = jnp.exp2((b - peak) * factor)
        self_weight = jnp.exp2((self_score - peak) * factor)
        mass = jnp.sum(a + b, axis=1, keepdims=True) + self_weight
        mixed = dot(a.astype(BF), values[p]) + dot(b.astype(BF), other_values[p])
        mixed = mixed + self_weight.astype(BF).astype(F32) * fresh_v
        mixed = (mixed / mass).astype(BF)
        for h in range(heads):
            sorted_rows[p * rows : (p + 1) * rows, h * HD : (h + 1) * HD] = mixed[h * rows : (h + 1) * rows]
        sorted_rows[p * rows : (p + 1) * rows, width : width + LANES] = log_stats(peak, mass, factor, heads, rows)

    tall = (suf.shape[0] - own) // 2
    span = tall // own

    def suffix_part(rel, cache):
        qs = heads_down(own_q[rel * own : (rel + 1) * own], heads)
        s = dot_t(qs, cache[:tall])
        row = lax.broadcasted_iota(jnp.int32, (own, 1), 0)
        row = jnp.concatenate([row * span] * heads, axis=0)
        length = cache[2 * tall :, :1].astype(F32).astype(jnp.int32)
        length = jnp.concatenate([length] * heads, axis=0)
        t = lax.broadcasted_iota(jnp.int32, s.shape, 1) - row
        s = jnp.where((t >= 0) & (t < length), s, NEG)
        top = jnp.max(s, axis=1, keepdims=True)
        w = jnp.exp2((s - top) * factor)
        m = jnp.sum(w, axis=1, keepdims=True)
        o = (dot(w.astype(BF), cache[tall : 2 * tall]) / m).astype(BF)
        at = pl.ds(pl.multiple_of((core ^ rel) * own, own), own)
        for h in range(heads):
            suffix_out[at, h * HD : (h + 1) * HD] = o[h * own : (h + 1) * own]
        suffix_out[at, width : width + LANES] = log_stats(top, m, factor, heads, own)

    pending = score(0)
    for p in range(prompts):
        following = score(p + 1) if p + 1 < prompts else None
        finish(p, pending)
        if p in (1, 4):
            suffix_part(*((0, suf) if p == 1 else (1, other_suf)))
        pending = following

    place = lax.broadcasted_iota(jnp.int32, (total, total), 1)
    to_row = jnp.where(place == rank_of[...], 1.0, 0.0).astype(BF)
    placed = dot(to_row, sorted_rows[...]).astype(BF)
    n = out.shape[1]
    for i in range(out.shape[0]):
        out[i] = placed[i * n : (i + 1) * n]


def stage_kernel(home, out, landed):
    copy = pltpu.make_async_copy(home, out, landed)
    copy.start()
    copy.wait()


def join_kernel(heads, parts, suffix, out):
    width = heads * HD
    count = parts.shape[0]
    stats = [join_stats(parts[i, :, width : width + LANES]) for i in range(count)]
    stats.append(join_stats(suffix[:, width : width + LANES]))
    top = functools.reduce(jnp.maximum, stats)
    grown = [jnp.exp2(s - top) for s in stats]
    total = functools.reduce(jnp.add, grown)
    share = [e / total for e in grown]
    for h in range(heads):
        cut = slice(h * HD, (h + 1) * HD)
        o = suffix[:, cut].astype(F32) * share[count][:, h : h + 1]
        for i in range(count):
            o = o + parts[i, :, cut].astype(F32) * share[i][:, h : h + 1]
        o = o.astype(BF)
        for i in range(out.shape[0]):
            out[i, :, cut] = o


def project_kernel(spot, mine, partner, w0, w1, w2, w3, out):
    core, group = spot[0], spot[1]
    out[...] = jnp.zeros_like(out)
    depth = mine.shape[1]
    near = pl.ds(pl.multiple_of(core * depth, depth), depth)
    far = pl.ds(pl.multiple_of((1 - core) * depth, depth), depth)
    n = out.shape[1]
    for rel, w in enumerate((w0, w1, w2, w3)):
        y = (dot(mine[...], w[near, :]) + dot(partner[...], w[far, :])).astype(BF)
        for high in range(2):
            out[((group % 2) * 2 + high) * 4 + (group ^ rel)] = y[high * n : (high + 1) * n]


def plane_kernel(spot, parts, keep, send):
    sums = []
    for top in range(2):
        terms = [parts[y * 4 + top * 2 + g].astype(F32) for y in range(4) for g in range(2)]
        sums.append(functools.reduce(jnp.add, terms))
    upper = spot[2] == 1
    keep[...] = jnp.where(upper, sums[1], sums[0])
    send[...] = jnp.where(upper, sums[0], sums[1]).astype(BF)


VMEM = pl.BlockSpec(memory_space=pltpu.VMEM)
SMEM = pl.BlockSpec(memory_space=pltpu.SMEM)


def body(counts, prompt_of, queries, new_kv, prompt_keys, prompt_values, suffix_keys, suffix_values, gen_len, out_weight):
    me = lax.axis_index("seq")
    core, chip = me & 1, me >> 1
    group = lax.axis_index("rep")
    upper = lax.axis_index("tp") >> 2
    capacity, width = queries.shape[1:]
    heads = width // HD // 2
    half = heads * HD
    per_device = gen_len.shape[1]
    seq_count = lax.axis_size("seq")
    chips = seq_count // 2
    total = per_device * seq_count
    prompts, _ = prompt_keys.shape[1:3]
    block = total // prompts
    line = [[2 * i + c for i in range(chips)] for c in range(2)]

    halves = queries[0][:, :half], queries[0][:, half:]
    low = core == 0
    mine = jnp.where(low, halves[0], halves[1])
    theirs = jnp.where(low, halves[1], halves[0])
    far_chip = swap(mine, "seq", 8)
    far_cross = swap(theirs, "seq", 9)
    near_core = swap(theirs, "seq", 1)
    slots = jnp.concatenate([mine, near_core, far_chip, far_cross], axis=0)

    spot = jnp.stack([core, group, upper, chip]).astype(jnp.int32)
    new_rows, sk, sv, gens = new_kv[0], suffix_keys[0], suffix_values[0], gen_len[0]
    keys, values, weight, tally, prompt = prompt_keys[0], prompt_values[0], out_weight, counts, prompt_of
    small = jnp.pad(new_rows.reshape(capacity, 2 * HD), ((0, per_device), (0, 0)))
    lengths = jnp.broadcast_to(gens.astype(BF)[:, None], (per_device, HD))
    suffix = jnp.concatenate([sk.reshape(-1, HD), sv.reshape(-1, HD), lengths], axis=0)
    slots = jnp.concatenate([slots, swap(slots, "seq", 4)], axis=0)
    far_slots = swap(slots, "seq", 2)
    other_small = swap(small, "seq", 1)
    other_suffix = swap(suffix, "seq", 1)
    other_keys = swap(keys, "seq", 1)
    home = pltpu.with_memory_space_constraint(values, pltpu.HBM)
    staged = pl.pallas_call(
        stage_kernel,
        out_shape=jax.ShapeDtypeStruct(values.shape, BF),
        in_specs=[pl.BlockSpec(memory_space=pltpu.HBM)],
        out_specs=VMEM,
        scratch_shapes=[pltpu.SemaphoreType.DMA],
        compiler_params=pltpu.CompilerParams(vmem_limit_bytes=8 << 20),
        name="stage",
    )(home)
    other_values = swap(values, "seq", 1)
    weights = [weight]
    for bit in (1, 2, 3):
        weights.append(swap(weight, "rep", bit))
    tables = pl.pallas_call(
        functools.partial(order_kernel, block, capacity),
        out_shape=[
            jax.ShapeDtypeStruct((total, 1), jnp.int32),
            jax.ShapeDtypeStruct((total, 1), jnp.int32),
            jax.ShapeDtypeStruct((2 * per_device, 1), jnp.int32),
        ],
        in_specs=[SMEM, SMEM, VMEM],
        out_specs=[VMEM] * 3,
        compiler_params=pltpu.CompilerParams(vmem_limit_bytes=8 << 20),
        cost_estimate=pl.CostEstimate(flops=1 << 20, bytes_accessed=1 << 18, transcendentals=0),
        name="order",
    )(spot, tally, prompt)

    packed = half + LANES
    parts, own_part = pl.pallas_call(
        functools.partial(attend_kernel, heads),
        out_shape=[
            jax.ShapeDtypeStruct((chips, total // chips, packed), BF),
            jax.ShapeDtypeStruct((2 * per_device, packed), BF),
        ],
        in_specs=[SMEM] + [VMEM] * 13,
        out_specs=[VMEM] * 2,
        scratch_shapes=[
            pltpu.VMEM((total, packed), BF),
            pltpu.VMEM((prompts, block * heads, HD), BF),
            pltpu.VMEM((total, 2 * HD), F32),
        ],
        compiler_params=pltpu.CompilerParams(vmem_limit_bytes=24 << 20),
        name="attend",
    )(
        spot,
        *tables,
        slots,
        far_slots,
        small,
        other_small,
        keys,
        other_keys,
        staged,
        other_values,
        suffix,
        other_suffix,
    )
    parts = lax.all_to_all(parts, "seq", 0, 0, axis_index_groups=line, tiled=True)
    spread = pl.pallas_call(
        functools.partial(join_kernel, heads),
        out_shape=jax.ShapeDtypeStruct((chips, 2 * per_device, half), BF),
        in_specs=[VMEM] * 2,
        out_specs=VMEM,
        compiler_params=pltpu.CompilerParams(vmem_limit_bytes=8 << 20),
        name="join",
    )(parts, own_part)
    attended = lax.all_to_all(spread, "seq", 0, 0, axis_index_groups=line, tiled=True).reshape(total, half)
    partner = swap(attended, "seq", 1)
    columns = out_weight.shape[1]
    plane = [[(z * 4 + y) * 4 + x for y in range(4) for x in range(4)] for z in range(2)]
    products = pl.pallas_call(
        project_kernel,
        out_shape=jax.ShapeDtypeStruct((16, total // 2, columns), BF),
        in_specs=[SMEM] + [VMEM] * 6,
        out_specs=VMEM,
        compiler_params=pltpu.CompilerParams(vmem_limit_bytes=8 << 20),
        name="project",
    )(spot, attended, partner, *weights)
    products = lax.all_to_all(products, ("tp", "rep"), 0, 0, axis_index_groups=plane, tiled=True)
    keep, send = pl.pallas_call(
        plane_kernel,
        out_shape=[
            jax.ShapeDtypeStruct((total // 2, columns), F32),
            jax.ShapeDtypeStruct((total // 2, columns), BF),
        ],
        in_specs=[SMEM, VMEM],
        out_specs=[VMEM] * 2,
        compiler_params=pltpu.CompilerParams(vmem_limit_bytes=8 << 20),
        name="plane",
    )(spot, products)
    return (keep + swap(send, "tp", 4).astype(F32)).astype(BF)


def solution(mesh):
    in_specs = (
        P("rep", None),
        P("rep", None),
        P("rep", "seq", "tp"),
        P("rep", "seq", None, "tp"),
        P("rep", None, "seq", "tp"),
        P("rep", None, "seq", "tp"),
        P("rep", "seq", None, "tp"),
        P("rep", "seq", None, "tp"),
        P("rep", "seq"),
        P("tp", ("seq", "rep")),
    )
    out_specs = P("tp", ("seq", "rep"))
    return jax.shard_map(body, mesh=mesh, in_specs=in_specs, out_specs=out_specs, check_vma=False)
```

time: 155 us -> 147 us (0.948)
  waiting for transfers between devices: 36.2 us -> 30.1 us
  other arithmetic: 7.4 us -> 3.56 us
  starting transfers between devices: 48.7 us -> 52.4 us
    ppermute x13 -> x14, waiting for transfers between devices: 28.8 us -> 23.9 us  [swap(): return lax.ppermute(x, axis, [(i, i ^ bit) for i in range(size)])]
    ppermute x13 -> x14, starting transfers between devices: 44.2 us -> 47.9 us  [swap(): return lax.ppermute(x, axis, [(i, i ^ bit) for i in range(size)])]
    reduce_sum x4 -> x0, other arithmetic: 2.01 us -> none  [the longest x1 0.93 us: body(): rank = prompt * block + jnp.sum(before.astype(jnp.int32), axis=1)]
    pallas_call x1 -> x3, Pallas kernels: 10.6 us -> 9.48 us  [the longest x1 6.84 us: body(): pl.pallas_call(functools.partial(attend_kernel, heads), out_shape=[jax.Sh...]
  transfers between devices with their start and end apart: 14 -> 15, of which waited for: 6 -> 6; matrix products, arithmetic and copies ran while one was open for 5% -> 2% of each run, Pallas kernels for 0% -> 2%
where the time goes in v3:
time: 147 us; the launch traced here: 144 us
  starting transfers between devices  52.4 us (36%)
  blocking collectives  44.2 us (30%)
  waiting for transfers between devices  30.1 us (20%)
  Pallas kernels  12.4 us (8%)
  other arithmetic  3.56 us (2%)
    ppermute x14, starting transfers between devices, swap(): return lax.ppermute(x, axis, [(i, i ^ bit) for i in range(size)])  47.9 us
    all_to_all x1, blocking collectives, body(): lax.all_to_all(parts, 'seq', 0, 0, axis_index_groups=line, tiled=True)  28.4 us
    ppermute x14, waiting for transfers between devices, swap(): return lax.ppermute(x, axis, [(i, i ^ bit) for i in range(size)])  23.9 us
    all_to_all x1, blocking collectives, body(): lax.all_to_all(products, ('tp', 'rep'), 0, 0, axis_index_groups=plane, ti...  15.8 us
    pallas_call x1, Pallas kernels, body(): pl.pallas_call(functools.partial(attend_kernel, heads), out_shape=[jax.Sh...  6.84 us
    all_to_all x1, waiting for transfers between devices, body(): lax.all_to_all(spread, 'seq', 0, 0, axis_index_groups=line, tiled=True)  6.16 us
    all_to_all x1, starting transfers between devices, body(): lax.all_to_all(spread, 'seq', 0, 0, axis_index_groups=line, tiled=True)  4.45 us
  transfers between devices with their start and end apart: 15, of which 6 were waited for; matrix products, arithmetic and copies ran while one was open for 2% of the time, Pallas kernels for 2%

profile of v3, /device:TPU:6, one launch (start us, length us, event | category | flops | bytes accessed | tf_op | source)
XLA Modules:
  0.0 143.9 jit_solution(7694199980328699260)
XLA Ops:
  0.0 2.0 %collective-permute-start.6 = (bf16[8,1024,128]{2,1,0:T(8,128)(2,1)}, bf16[8,1024,128]{2,1,0:T(8,128)(2,1)S(1)}, u32[]{:S(2)}, u32[]{:S(2)}) collective-permute-start(bf16[8,1024,128]{2,1,0:T(8,128)(2,1)} %bitcast.17), channel_id=1, source_target_pairs={{0,32},{32,0},{64,96},{96,64},{128,160},{160,128},{192,224},{224,1... | collective-permute-start | bytes 6291464 | tf_op jit(solution)/shard_map/ppermute | solution.py:21
  2.1 2.4 %collective-permute-start.7 = (bf16[8,1024,128]{2,1,0:T(8,128)(2,1)}, bf16[8,1024,128]{2,1,0:T(8,128)(2,1)}, u32[]{:S(2)}, u32[]{:S(2)}) collective-permute-start(bf16[8,1024,128]{2,1,0:T(8,128)(2,1)} %bitcast.21), channel_id=1, source_target_pairs={{0,32},{32,0},{64,96},{96,64},{128,160},{160,128},{192,224},{224,1... | collective-permute-start | bytes 6291464 | tf_op jit(solution)/shard_map/ppermute | solution.py:21
  5.3 1.9 %collective-permute-start = (bf16[40,512]{1,0:T(8,128)(2,1)S(1)}, bf16[40,512]{1,0:T(8,128)(2,1)S(1)}, u32[]{:S(2)}, u32[]{:S(2)}) collective-permute-start(bf16[40,512]{1,0:T(8,128)(2,1)S(1)} %get-tuple-element.21), channel_id=1, source_target_pairs={{0,32},{32,0},{64,96},{96,64},{128,160},{160,128},{192,224},{224,1... | collective-permute-start | bytes 122888 | tf_op jit(solution)/shard_map/ppermute | solution.py:21
  7.2 9.2 %collective-permute-start.2 = (bf16[40,512]{1,0:T(8,128)(2,1)S(1)}, bf16[40,512]{1,0:T(8,128)(2,1)S(1)}, u32[]{:S(2)}, u32[]{:S(2)}) collective-permute-start(bf16[40,512]{1,0:T(8,128)(2,1)S(1)} %get-tuple-element.21), channel_id=1, source_target_pairs={{0,288},{32,256},{64,352},{96,320},{128,416},{160,384},{192,480},{... | collective-permute-start | bytes 122888 | tf_op jit(solution)/shard_map/ppermute | solution.py:21
  16.4 1.9 %collective-permute-start.1 = (bf16[40,512]{1,0:T(8,128)(2,1)S(1)}, bf16[40,512]{1,0:T(8,128)(2,1)S(1)}, u32[]{:S(2)}, u32[]{:S(2)}) collective-permute-start(bf16[40,512]{1,0:T(8,128)(2,1)S(1)} %get-tuple-element.20), channel_id=1, source_target_pairs={{0,256},{32,288},{64,320},{96,352},{128,384},{160,416},{192,448},{... | collective-permute-start | bytes 122888 | tf_op jit(solution)/shard_map/ppermute | solution.py:21
  20.4 2.0 %collective-permute-start.8 = (bf16[2064,128]{1,0:T(8,128)(2,1)S(1)}, bf16[2064,128]{1,0:T(8,128)(2,1)S(1)}, u32[]{:S(2)}, u32[]{:S(2)}) collective-permute-start(bf16[2064,128]{1,0:T(8,128)(2,1)S(1)} %maximum_maximum_fusion.suf), channel_id=1, source_target_pairs={{0,32},{32,0},{64,96},{96,64},{128,160},{160,128},{192,224},{224,1... | collective-permute-start | bytes 1585160 | tf_op jit(solution)/shard_map/ppermute | solution.py:21
  22.4 3.8 %collective-permute-done.1 = bf16[40,512]{1,0:T(8,128)(2,1)S(1)} collective-permute-done((bf16[40,512]{1,0:T(8,128)(2,1)S(1)}, bf16[40,512]{1,0:T(8,128)(2,1)S(1)}, u32[]{:S(2)}, u32[]{:S(2)}) %collective-permute-start.1) | collective-permute-done | bytes 40992 | tf_op jit(solution)/shard_map/ppermute | solution.py:21
  26.3 5.2 %collective-permute-start.3 = (bf16[160,512]{1,0:T(8,128)(2,1)S(1)}, bf16[160,512]{1,0:T(8,128)(2,1)S(1)}, u32[]{:S(2)}, u32[]{:S(2)}) collective-permute-start(bf16[160,512]{1,0:T(8,128)(2,1)S(1)} %pad_maximum_fusion), channel_id=1, source_target_pairs={{0,128},{32,160},{64,192},{96,224},{128,0},{160,32},{192,64},{224,... | collective-permute-start | bytes 491528 | tf_op jit(solution)/shard_map/ppermute | solution.py:21
  31.5 6.7 %collective-permute-done.3 = bf16[160,512]{1,0:T(8,128)(2,1)S(1)} collective-permute-done((bf16[160,512]{1,0:T(8,128)(2,1)S(1)}, bf16[160,512]{1,0:T(8,128)(2,1)S(1)}, u32[]{:S(2)}, u32[]{:S(2)}) %collective-permute-start.3) | collective-permute-done | bytes 163872 | tf_op jit(solution)/shard_map/ppermute | solution.py:21
  38.2 2.6 %collective-permute-start.4 = (bf16[320,512]{1,0:T(8,128)(2,1)S(1)}, bf16[320,512]{1,0:T(8,128)(2,1)}, u32[]{:S(2)}, u32[]{:S(2)}) collective-permute-start(bf16[320,512]{1,0:T(8,128)(2,1)S(1)} %constant_dynamic-update-slice_fusion.near), channel_id=1, source_target_pairs={{0,64},{32,96},{64,0},{96,32},{128,192},{160,224},{192,128},{224,1... | collective-permute-start | bytes 983048 | tf_op jit(solution)/shard_map/ppermute | solution.py:21
  40.9 1.9 %collective-permute-start.5 = (bf16[56,256]{1,0:T(8,128)(2,1)S(1)}, bf16[56,256]{1,0:T(8,128)(2,1)S(1)}, u32[]{:S(2)}, u32[]{:S(2)}) collective-permute-start(bf16[56,256]{1,0:T(8,128)(2,1)S(1)} %pad.4.small), channel_id=1, source_target_pairs={{0,32},{32,0},{64,96},{96,64},{128,160},{160,128},{192,224},{224,1... | collective-permute-start | bytes 86024 | tf_op jit(solution)/shard_map/ppermute | solution.py:21
  45.6 3.0 %collective-permute-done.4.far = bf16[320,512]{1,0:T(8,128)(2,1)} collective-permute-done((bf16[320,512]{1,0:T(8,128)(2,1)S(1)}, bf16[320,512]{1,0:T(8,128)(2,1)}, u32[]{:S(2)}, u32[]{:S(2)}) %collective-permute-start.4) | collective-permute-done | bytes 327712 | tf_op jit(solution)/shard_map/ppermute | solution.py:21
  48.6 6.8 %attend.1 = (bf16[8,32,640]{2,1,0:T(8,128)(2,1)S(1)}, bf16[32,640]{1,0:T(8,128)(2,1)S(1)}) custom-call(s32[4]{0:T(128)S(1)} %pad_add_fusion.spot, s32[256,1]{1,0:T(8,128)S(1)} %get-tuple-element.12.slot_of, s32[256,1]{1,0:T(8,128)S(1)} %get-tuple-element.13.rank_of, s32[32,1]{1,0:T(8,128)S(1)} %get-tuple-element.14.own_slot, ...), custom_call_target="tpu_custom_call" | custom-call | tf_op jit(solution)/shard_map/attend/pallas_call | solution.py:303
  55.5 28.4 %all_to_all.15.parts = bf16[8,32,640]{2,1,0:T(8,128)(2,1)S(1)} all-to-all(bf16[8,32,640]{2,1,0:T(8,128)(2,1)S(1)} %get-tuple-element.15), channel_id=1, replica_groups={{0,64,128,192,256,320,384,448},{32,96,160,224,288,352,416,480},{1,65,12..., dimensions={0} | all-to-all | bytes 655360 | tf_op jit(solution)/shard_map/all_to_all | solution.py:332
  85.0 4.5 %all-to-all-start.1 = ((bf16[8,32,512]{2,1,0:T(8,128)(2,1)}), bf16[8,32,512]{2,1,0:T(8,128)(2,1)S(1)}, u32[]{:S(2)}, u32[]{:S(2)}) async-start(bf16[8,32,512]{2,1,0:T(8,128)(2,1)} %join.1), calls=%async_computation.1 | async-start | bytes 524288 | tf_op jit(solution)/shard_map/all_to_all | solution.py:341
  89.4 2.7 %collective-permute-start.10 = (bf16[1024,128]{1,0:T(8,128)(2,1)}, bf16[1024,128]{1,0:T(8,128)(2,1)S(1)}, u32[]{:S(2)}, u32[]{:S(2)}) collective-permute-start(bf16[1024,128]{1,0:T(8,128)(2,1)} %w0.1), channel_id=1, source_target_pairs={{0,1},{1,0},{2,3},{3,2},{4,5},{5,4},{6,7},{7,6},{8,9},{9,8},{10,11... | collective-permute-start | bytes 786440 | tf_op jit(solution)/shard_map/ppermute | solution.py:21
  92.1 3.1 %collective-permute-start.11 = (bf16[1024,128]{1,0:T(8,128)(2,1)}, bf16[1024,128]{1,0:T(8,128)(2,1)S(1)}, u32[]{:S(2)}, u32[]{:S(2)}) collective-permute-start(bf16[1024,128]{1,0:T(8,128)(2,1)} %w0.1), channel_id=1, source_target_pairs={{0,2},{1,3},{2,0},{3,1},{4,6},{5,7},{6,4},{7,5},{8,10},{9,11},{10,... | collective-permute-start | bytes 786440 | tf_op jit(solution)/shard_map/ppermute | solution.py:21
  95.2 4.6 %collective-permute-start.12 = (bf16[1024,128]{1,0:T(8,128)(2,1)}, bf16[1024,128]{1,0:T(8,128)(2,1)S(1)}, u32[]{:S(2)}, u32[]{:S(2)}) collective-permute-start(bf16[1024,128]{1,0:T(8,128)(2,1)} %w0.1), channel_id=1, source_target_pairs={{0,3},{1,2},{2,1},{3,0},{4,7},{5,6},{6,5},{7,4},{8,11},{9,10},{10,... | collective-permute-start | bytes 786440 | tf_op jit(solution)/shard_map/ppermute | solution.py:21
  99.9 6.2 %all-to-all-done.1 = bf16[8,32,512]{2,1,0:T(8,128)(2,1)S(1)} async-done(((bf16[8,32,512]{2,1,0:T(8,128)(2,1)}), bf16[8,32,512]{2,1,0:T(8,128)(2,1)S(1)}, u32[]{:S(2)}, u32[]{:S(2)}) %all-to-all-start.1) | async-done | bytes 262176 | tf_op jit(solution)/shard_map/all_to_all | solution.py:341
  106.0 1.9 %collective-permute-start.9 = (bf16[256,512]{1,0:T(8,128)(2,1)S(1)}, bf16[256,512]{1,0:T(8,128)(2,1)S(1)}, u32[]{:S(2)}, u32[]{:S(2)}) collective-permute-start(bf16[256,512]{1,0:T(8,128)(2,1)S(1)} %bitcast.19), channel_id=1, source_target_pairs={{0,32},{32,0},{64,96},{96,64},{128,160},{160,128},{192,224},{224,1... | collective-permute-start | bytes 786440 | tf_op jit(solution)/shard_map/ppermute | solution.py:21
  108.0 2.1 %collective-permute-done.12.w3 = bf16[1024,128]{1,0:T(8,128)(2,1)S(1)} collective-permute-done((bf16[1024,128]{1,0:T(8,128)(2,1)}, bf16[1024,128]{1,0:T(8,128)(2,1)S(1)}, u32[]{:S(2)}, u32[]{:S(2)}) %collective-permute-start.12) | collective-permute-done | bytes 262176 | tf_op jit(solution)/shard_map/ppermute | solution.py:21
  112.3 15.8 %all_to_all.16.parts = bf16[16,128,128]{2,1,0:T(8,128)(2,1)S(1)} all-to-all(bf16[16,128,128]{2,1,0:T(8,128)(2,1)S(1)} %project.1), channel_id=1, replica_groups={{0,1,2,3,4,5,6,7,8,9,10,11,12,13,14,15},{16,17,18,19,20,21,22,23,24,25,..., dimensions={0} | all-to-all | bytes 1048576 | tf_op jit(solution)/shard_map/all_to_all | solution.py:353
  128.7 6.4 %collective-permute-start.13 = (bf16[128,128]{1,0:T(8,128)(2,1)S(1)}, bf16[128,128]{1,0:T(8,128)(2,1)S(1)}, u32[]{:S(2)}, u32[]{:S(2)}) collective-permute-start(bf16[128,128]{1,0:T(8,128)(2,1)S(1)} %get-tuple-element.18), channel_id=1, source_target_pairs={{0,16},{4,20},{8,24},{12,28},{16,0},{20,4},{24,8},{28,12},{1,17},{... | collective-permute-start | bytes 98312 | tf_op jit(solution)/shard_map/ppermute | solution.py:21
  135.1 8.2 %collective-permute-done.13 = bf16[128,128]{1,0:T(8,128)(2,1)S(1)} collective-permute-done((bf16[128,128]{1,0:T(8,128)(2,1)S(1)}, bf16[128,128]{1,0:T(8,128)(2,1)S(1)}, u32[]{:S(2)}, u32[]{:S(2)}) %collective-permute-start.13) | collective-permute-done | bytes 32800 | tf_op jit(solution)/shard_map/ppermute | solution.py:21
  (37 shorter events, 10.2 us)
Async XLA Ops:
  0.0 40.9 %copy-start.4 = (bf16[1,40,2,128]{3,2,1,0:T(2,128)(2,1)S(1)}, bf16[1,40,2,128]{3,2,1,0:T(2,128)(2,1)}, u32[]{:S(2)}) copy-start(bf16[1,40,2,128]{3,2,1,0:T(2,128)(2,1)} %param.13) | copy-start | bytes 61444
  0.0 48.6 %collective-permute-start.6 = (bf16[8,1024,128]{2,1,0:T(8,128)(2,1)}, bf16[8,1024,128]{2,1,0:T(8,128)(2,1)S(1)}, u32[]{:S(2)}, u32[]{:S(2)}) collective-permute-start(bf16[8,1024,128]{2,1,0:T(8,128)(2,1)} %bitcast.17), channel_id=1, source_target_pairs={{0,32},{32,0},{64,96},{96,64},{128,160},{160,128},{192,224},{224,1... | collective-permute-start | bytes 6291464 | tf_op jit(solution)/shard_map/ppermute | solution.py:21
  2.1 46.6 %collective-permute-start.7 = (bf16[8,1024,128]{2,1,0:T(8,128)(2,1)}, bf16[8,1024,128]{2,1,0:T(8,128)(2,1)}, u32[]{:S(2)}, u32[]{:S(2)}) collective-permute-start(bf16[8,1024,128]{2,1,0:T(8,128)(2,1)} %bitcast.21), channel_id=1, source_target_pairs={{0,32},{32,0},{64,96},{96,64},{128,160},{160,128},{192,224},{224,1... | collective-permute-start | bytes 6291464 | tf_op jit(solution)/shard_map/ppermute | solution.py:21
  5.3 15.1 %collective-permute-start = (bf16[40,512]{1,0:T(8,128)(2,1)S(1)}, bf16[40,512]{1,0:T(8,128)(2,1)S(1)}, u32[]{:S(2)}, u32[]{:S(2)}) collective-permute-start(bf16[40,512]{1,0:T(8,128)(2,1)S(1)} %get-tuple-element.21), channel_id=1, source_target_pairs={{0,32},{32,0},{64,96},{96,64},{128,160},{160,128},{192,224},{224,1... | collective-permute-start | bytes 122888 | tf_op jit(solution)/shard_map/ppermute | solution.py:21
  7.2 19.0 %collective-permute-start.2 = (bf16[40,512]{1,0:T(8,128)(2,1)S(1)}, bf16[40,512]{1,0:T(8,128)(2,1)S(1)}, u32[]{:S(2)}, u32[]{:S(2)}) collective-permute-start(bf16[40,512]{1,0:T(8,128)(2,1)S(1)} %get-tuple-element.21), channel_id=1, source_target_pairs={{0,288},{32,256},{64,352},{96,320},{128,416},{160,384},{192,480},{... | collective-permute-start | bytes 122888 | tf_op jit(solution)/shard_map/ppermute | solution.py:21
  16.4 9.8 %collective-permute-start.1 = (bf16[40,512]{1,0:T(8,128)(2,1)S(1)}, bf16[40,512]{1,0:T(8,128)(2,1)S(1)}, u32[]{:S(2)}, u32[]{:S(2)}) collective-permute-start(bf16[40,512]{1,0:T(8,128)(2,1)S(1)} %get-tuple-element.20), channel_id=1, source_target_pairs={{0,256},{32,288},{64,320},{96,352},{128,384},{160,416},{192,448},{... | collective-permute-start | bytes 122888 | tf_op jit(solution)/shard_map/ppermute | solution.py:21
  20.4 25.2 %collective-permute-start.8 = (bf16[2064,128]{1,0:T(8,128)(2,1)S(1)}, bf16[2064,128]{1,0:T(8,128)(2,1)S(1)}, u32[]{:S(2)}, u32[]{:S(2)}) collective-permute-start(bf16[2064,128]{1,0:T(8,128)(2,1)S(1)} %maximum_maximum_fusion.suf), channel_id=1, source_target_pairs={{0,32},{32,0},{64,96},{96,64},{128,160},{160,128},{192,224},{224,1... | collective-permute-start | bytes 1585160 | tf_op jit(solution)/shard_map/ppermute | solution.py:21
  26.3 11.9 %collective-permute-start.3 = (bf16[160,512]{1,0:T(8,128)(2,1)S(1)}, bf16[160,512]{1,0:T(8,128)(2,1)S(1)}, u32[]{:S(2)}, u32[]{:S(2)}) collective-permute-start(bf16[160,512]{1,0:T(8,128)(2,1)S(1)} %pad_maximum_fusion), channel_id=1, source_target_pairs={{0,128},{32,160},{64,192},{96,224},{128,0},{160,32},{192,64},{224,... | collective-permute-start | bytes 491528 | tf_op jit(solution)/shard_map/ppermute | solution.py:21
  38.2 10.4 %collective-permute-start.4 = (bf16[320,512]{1,0:T(8,128)(2,1)S(1)}, bf16[320,512]{1,0:T(8,128)(2,1)}, u32[]{:S(2)}, u32[]{:S(2)}) collective-permute-start(bf16[320,512]{1,0:T(8,128)(2,1)S(1)} %constant_dynamic-update-slice_fusion.near), channel_id=1, source_target_pairs={{0,64},{32,96},{64,0},{96,32},{128,192},{160,224},{192,128},{224,1... | collective-permute-start | bytes 983048 | tf_op jit(solution)/shard_map/ppermute | solution.py:21
  40.9 4.7 %collective-permute-start.5 = (bf16[56,256]{1,0:T(8,128)(2,1)S(1)}, bf16[56,256]{1,0:T(8,128)(2,1)S(1)}, u32[]{:S(2)}, u32[]{:S(2)}) collective-permute-start(bf16[56,256]{1,0:T(8,128)(2,1)S(1)} %pad.4.small), channel_id=1, source_target_pairs={{0,32},{32,0},{64,96},{96,64},{128,160},{160,128},{192,224},{224,1... | collective-permute-start | bytes 86024 | tf_op jit(solution)/shard_map/ppermute | solution.py:21
  42.9 1.8 %copy-start.2 = (s32[1,256]{1,0:T(1,128)S(1)}, s32[1,256]{1,0:T(1,128)}, u32[]{:S(2)}) copy-start(s32[1,256]{1,0:T(1,128)} %prompt.1) | copy-start | bytes 3076
  42.9 1.8 %copy-start.3 = (s32[1,16]{1,0:T(1,128)S(1)}, s32[1,16]{1,0:T(1,128)}, u32[]{:S(2)}) copy-start(s32[1,16]{1,0:T(1,128)} %counts.1) | copy-start | bytes 196
  42.9 5.7 %copy-start = (bf16[1,8,1024,128]{3,2,1,0:T(8,128)(2,1)S(1)}, bf16[1,8,1024,128]{3,2,1,0:T(8,128)(2,1)}, u32[]{:S(2)}) copy-start(bf16[1,8,1024,128]{3,2,1,0:T(8,128)(2,1)} %param.14) | copy-start | bytes 6291460
  85.0 21.1 %all-to-all-start.1 = ((bf16[8,32,512]{2,1,0:T(8,128)(2,1)}), bf16[8,32,512]{2,1,0:T(8,128)(2,1)S(1)}, u32[]{:S(2)}, u32[]{:S(2)}) async-start(bf16[8,32,512]{2,1,0:T(8,128)(2,1)} %join.1), calls=%async_computation.1 | async-start | bytes 524288 | tf_op jit(solution)/shard_map/all_to_all | solution.py:341
  89.4 18.5 %collective-permute-start.10 = (bf16[1024,128]{1,0:T(8,128)(2,1)}, bf16[1024,128]{1,0:T(8,128)(2,1)S(1)}, u32[]{:S(2)}, u32[]{:S(2)}) collective-permute-start(bf16[1024,128]{1,0:T(8,128)(2,1)} %w0.1), channel_id=1, source_target_pairs={{0,1},{1,0},{2,3},{3,2},{4,5},{5,4},{6,7},{7,6},{8,9},{9,8},{10,11... | collective-permute-start | bytes 786440 | tf_op jit(solution)/shard_map/ppermute | solution.py:21
  92.1 15.8 %collective-permute-start.11 = (bf16[1024,128]{1,0:T(8,128)(2,1)}, bf16[1024,128]{1,0:T(8,128)(2,1)S(1)}, u32[]{:S(2)}, u32[]{:S(2)}) collective-permute-start(bf16[1024,128]{1,0:T(8,128)(2,1)} %w0.1), channel_id=1, source_target_pairs={{0,2},{1,3},{2,0},{3,1},{4,6},{5,7},{6,4},{7,5},{8,10},{9,11},{10,... | collective-permute-start | bytes 786440 | tf_op jit(solution)/shard_map/ppermute | solution.py:21
  95.2 14.9 %collective-permute-start.12 = (bf16[1024,128]{1,0:T(8,128)(2,1)}, bf16[1024,128]{1,0:T(8,128)(2,1)S(1)}, u32[]{:S(2)}, u32[]{:S(2)}) collective-permute-start(bf16[1024,128]{1,0:T(8,128)(2,1)} %w0.1), channel_id=1, source_target_pairs={{0,3},{1,2},{2,1},{3,0},{4,7},{5,6},{6,5},{7,4},{8,11},{9,10},{10,... | collective-permute-start | bytes 786440 | tf_op jit(solution)/shard_map/ppermute | solution.py:21
  106.0 4.1 %collective-permute-start.9 = (bf16[256,512]{1,0:T(8,128)(2,1)S(1)}, bf16[256,512]{1,0:T(8,128)(2,1)S(1)}, u32[]{:S(2)}, u32[]{:S(2)}) collective-permute-start(bf16[256,512]{1,0:T(8,128)(2,1)S(1)} %bitcast.19), channel_id=1, source_target_pairs={{0,32},{32,0},{64,96},{96,64},{128,160},{160,128},{192,224},{224,1... | collective-permute-start | bytes 786440 | tf_op jit(solution)/shard_map/ppermute | solution.py:21
  110.1 1.0 copy-start.1
  128.7 14.6 %collective-permute-start.13 = (bf16[128,128]{1,0:T(8,128)(2,1)S(1)}, bf16[128,128]{1,0:T(8,128)(2,1)S(1)}, u32[]{:S(2)}, u32[]{:S(2)}) collective-permute-start(bf16[128,128]{1,0:T(8,128)(2,1)S(1)} %get-tuple-element.18), channel_id=1, source_target_pairs={{0,16},{4,20},{8,24},{12,28},{16,0},{20,4},{24,8},{28,12},{1,17},{... | collective-permute-start | bytes 98312 | tf_op jit(solution)/shard_map/ppermute | solution.py:21

commit v4 on v3

--- a/solution.py
+++ b/solution.py
@@ -208,14 +208,18 @@
             out[i, :, cut] = o
 
 
-def project_kernel(spot, mine, partner, w0, w1, w2, w3, out):
+def project_kernel(spot, mine, partner, home, w1, w2, w3, out, w0, landed):
     core, group = spot[0], spot[1]
+    fetch = pltpu.make_async_copy(home, w0, landed)
+    fetch.start()
     out[...] = jnp.zeros_like(out)
     depth = mine.shape[1]
     near = pl.ds(pl.multiple_of(core * depth, depth), depth)
     far = pl.ds(pl.multiple_of((1 - core) * depth, depth), depth)
     n = out.shape[1]
-    for rel, w in enumerate((w0, w1, w2, w3)):
+    for rel, w in ((1, w1), (2, w2), (3, w3), (0, w0)):
+        if rel == 0:
+            fetch.wait()
         y = (dot(mine[...], w[near, :]) + dot(partner[...], w[far, :])).astype(BF)
         for high in range(2):
             out[((group % 2) * 2 + high) * 4 + (group ^ rel)] = y[high * n : (high + 1) * n]
@@ -338,18 +342,20 @@
         compiler_params=pltpu.CompilerParams(vmem_limit_bytes=8 << 20),
         name="join",
     )(parts, own_part)
-    attended = lax.all_to_all(spread, "seq", 0, 0, axis_index_groups=line, tiled=True).reshape(total, half)
+    attended = lax.all_to_all(spread, "seq", 0, 0, axis_index_groups=line, tiled=True)
+    attended = attended.reshape(total, half)
     partner = swap(attended, "seq", 1)
     columns = out_weight.shape[1]
     plane = [[(z * 4 + y) * 4 + x for y in range(4) for x in range(4)] for z in range(2)]
     products = pl.pallas_call(
         project_kernel,
         out_shape=jax.ShapeDtypeStruct((16, total // 2, columns), BF),
-        in_specs=[SMEM] + [VMEM] * 6,
+        in_specs=[SMEM] + [VMEM] * 2 + [pl.BlockSpec(memory_space=pltpu.HBM)] + [VMEM] * 3,
         out_specs=VMEM,
+        scratch_shapes=[pltpu.VMEM(out_weight.shape, BF), pltpu.SemaphoreType.DMA],
         compiler_params=pltpu.CompilerParams(vmem_limit_bytes=8 << 20),
         name="project",
-    )(spot, attended, partner, *weights)
+    )(spot, attended, partner, pltpu.with_memory_space_constraint(out_weight, pltpu.HBM), *weights[1:])
     products = lax.all_to_all(products, ("tp", "rep"), 0, 0, axis_index_groups=plane, tiled=True)
     keep, send = pl.pallas_call(
         plane_kernel,

time: 147 us -> 146 us (level)
  no operation moved by 1% of the time
where the time goes in v4:
time: 146 us; the launch traced here: 144 us
  starting transfers between devices  52.4 us (36%)
  blocking collectives  44.2 us (30%)
  waiting for transfers between devices  30 us (21%)
  Pallas kernels  13 us (9%)
  other arithmetic  3.56 us (2%)
    ppermute x14, starting transfers between devices, swap(): return lax.ppermute(x, axis, [(i, i ^ bit) for i in range(size)])  48 us
    all_to_all x1, blocking collectives, body(): lax.all_to_all(parts, 'seq', 0, 0, axis_index_groups=line, tiled=True)  28.4 us
    ppermute x14, waiting for transfers between devices, swap(): return lax.ppermute(x, axis, [(i, i ^ bit) for i in range(size)])  23.9 us
    all_to_all x1, blocking collectives, body(): lax.all_to_all(products, ('tp', 'rep'), 0, 0, axis_index_groups=plane, ti...  15.8 us
    pallas_call x1, Pallas kernels, body(): pl.pallas_call(functools.partial(attend_kernel, heads), out_shape=[jax.Sh...  6.84 us
    all_to_all x1, waiting for transfers between devices, body(): lax.all_to_all(spread, 'seq', 0, 0, axis_index_groups=line, tiled=True)  6.16 us
    all_to_all x1, starting transfers between devices, body(): lax.all_to_all(spread, 'seq', 0, 0, axis_index_groups=line, tiled=True)  4.45 us
  transfers between devices with their start and end apart: 15, of which 6 were waited for; matrix products, arithmetic and copies ran while one was open for 2% of the time, Pallas kernels for 2%

profile of v4, /device:TPU:6, one launch (start us, length us, event | category | flops | bytes accessed | tf_op | source)
XLA Modules:
  0.0 143.5 jit_solution(5155154555499926266)
XLA Ops:
  0.0 2.0 %collective-permute-start.6 = (bf16[8,1024,128]{2,1,0:T(8,128)(2,1)}, bf16[8,1024,128]{2,1,0:T(8,128)(2,1)S(1)}, u32[]{:S(2)}, u32[]{:S(2)}) collective-permute-start(bf16[8,1024,128]{2,1,0:T(8,128)(2,1)} %bitcast.17), channel_id=1, source_target_pairs={{0,32},{32,0},{64,96},{96,64},{128,160},{160,128},{192,224},{224,1... | collective-permute-start | bytes 6291464 | tf_op jit(solution)/shard_map/ppermute | solution.py:21
  2.1 2.4 %collective-permute-start.7 = (bf16[8,1024,128]{2,1,0:T(8,128)(2,1)}, bf16[8,1024,128]{2,1,0:T(8,128)(2,1)}, u32[]{:S(2)}, u32[]{:S(2)}) collective-permute-start(bf16[8,1024,128]{2,1,0:T(8,128)(2,1)} %bitcast.21), channel_id=1, source_target_pairs={{0,32},{32,0},{64,96},{96,64},{128,160},{160,128},{192,224},{224,1... | collective-permute-start | bytes 6291464 | tf_op jit(solution)/shard_map/ppermute | solution.py:21
  5.3 1.9 %collective-permute-start = (bf16[40,512]{1,0:T(8,128)(2,1)S(1)}, bf16[40,512]{1,0:T(8,128)(2,1)S(1)}, u32[]{:S(2)}, u32[]{:S(2)}) collective-permute-start(bf16[40,512]{1,0:T(8,128)(2,1)S(1)} %get-tuple-element.21), channel_id=1, source_target_pairs={{0,32},{32,0},{64,96},{96,64},{128,160},{160,128},{192,224},{224,1... | collective-permute-start | bytes 122888 | tf_op jit(solution)/shard_map/ppermute | solution.py:21
  7.2 9.2 %collective-permute-start.2 = (bf16[40,512]{1,0:T(8,128)(2,1)S(1)}, bf16[40,512]{1,0:T(8,128)(2,1)S(1)}, u32[]{:S(2)}, u32[]{:S(2)}) collective-permute-start(bf16[40,512]{1,0:T(8,128)(2,1)S(1)} %get-tuple-element.21), channel_id=1, source_target_pairs={{0,288},{32,256},{64,352},{96,320},{128,416},{160,384},{192,480},{... | collective-permute-start | bytes 122888 | tf_op jit(solution)/shard_map/ppermute | solution.py:21
  16.4 1.9 %collective-permute-start.1 = (bf16[40,512]{1,0:T(8,128)(2,1)S(1)}, bf16[40,512]{1,0:T(8,128)(2,1)S(1)}, u32[]{:S(2)}, u32[]{:S(2)}) collective-permute-start(bf16[40,512]{1,0:T(8,128)(2,1)S(1)} %get-tuple-element.20), channel_id=1, source_target_pairs={{0,256},{32,288},{64,320},{96,352},{128,384},{160,416},{192,448},{... | collective-permute-start | bytes 122888 | tf_op jit(solution)/shard_map/ppermute | solution.py:21
  20.4 2.0 %collective-permute-start.8 = (bf16[2064,128]{1,0:T(8,128)(2,1)S(1)}, bf16[2064,128]{1,0:T(8,128)(2,1)S(1)}, u32[]{:S(2)}, u32[]{:S(2)}) collective-permute-start(bf16[2064,128]{1,0:T(8,128)(2,1)S(1)} %maximum_maximum_fusion.suf), channel_id=1, source_target_pairs={{0,32},{32,0},{64,96},{96,64},{128,160},{160,128},{192,224},{224,1... | collective-permute-start | bytes 1585160 | tf_op jit(solution)/shard_map/ppermute | solution.py:21
  22.4 3.8 %collective-permute-done.1 = bf16[40,512]{1,0:T(8,128)(2,1)S(1)} collective-permute-done((bf16[40,512]{1,0:T(8,128)(2,1)S(1)}, bf16[40,512]{1,0:T(8,128)(2,1)S(1)}, u32[]{:S(2)}, u32[]{:S(2)}) %collective-permute-start.1) | collective-permute-done | bytes 40992 | tf_op jit(solution)/shard_map/ppermute | solution.py:21
  26.3 5.2 %collective-permute-start.3 = (bf16[160,512]{1,0:T(8,128)(2,1)S(1)}, bf16[160,512]{1,0:T(8,128)(2,1)S(1)}, u32[]{:S(2)}, u32[]{:S(2)}) collective-permute-start(bf16[160,512]{1,0:T(8,128)(2,1)S(1)} %pad_maximum_fusion), channel_id=1, source_target_pairs={{0,128},{32,160},{64,192},{96,224},{128,0},{160,32},{192,64},{224,... | collective-permute-start | bytes 491528 | tf_op jit(solution)/shard_map/ppermute | solution.py:21
  31.5 6.7 %collective-permute-done.3 = bf16[160,512]{1,0:T(8,128)(2,1)S(1)} collective-permute-done((bf16[160,512]{1,0:T(8,128)(2,1)S(1)}, bf16[160,512]{1,0:T(8,128)(2,1)S(1)}, u32[]{:S(2)}, u32[]{:S(2)}) %collective-permute-start.3) | collective-permute-done | bytes 163872 | tf_op jit(solution)/shard_map/ppermute | solution.py:21
  38.2 2.6 %collective-permute-start.4 = (bf16[320,512]{1,0:T(8,128)(2,1)S(1)}, bf16[320,512]{1,0:T(8,128)(2,1)}, u32[]{:S(2)}, u32[]{:S(2)}) collective-permute-start(bf16[320,512]{1,0:T(8,128)(2,1)S(1)} %constant_dynamic-update-slice_fusion.near), channel_id=1, source_target_pairs={{0,64},{32,96},{64,0},{96,32},{128,192},{160,224},{192,128},{224,1... | collective-permute-start | bytes 983048 | tf_op jit(solution)/shard_map/ppermute | solution.py:21
  40.9 1.9 %collective-permute-start.5 = (bf16[56,256]{1,0:T(8,128)(2,1)S(1)}, bf16[56,256]{1,0:T(8,128)(2,1)S(1)}, u32[]{:S(2)}, u32[]{:S(2)}) collective-permute-start(bf16[56,256]{1,0:T(8,128)(2,1)S(1)} %pad.4.small), channel_id=1, source_target_pairs={{0,32},{32,0},{64,96},{96,64},{128,160},{160,128},{192,224},{224,1... | collective-permute-start | bytes 86024 | tf_op jit(solution)/shard_map/ppermute | solution.py:21
  45.6 3.0 %collective-permute-done.4.far = bf16[320,512]{1,0:T(8,128)(2,1)} collective-permute-done((bf16[320,512]{1,0:T(8,128)(2,1)S(1)}, bf16[320,512]{1,0:T(8,128)(2,1)}, u32[]{:S(2)}, u32[]{:S(2)}) %collective-permute-start.4) | collective-permute-done | bytes 327712 | tf_op jit(solution)/shard_map/ppermute | solution.py:21
  48.6 6.8 %attend.1 = (bf16[8,32,640]{2,1,0:T(8,128)(2,1)S(1)}, bf16[32,640]{1,0:T(8,128)(2,1)S(1)}) custom-call(s32[4]{0:T(128)S(1)} %pad_add_fusion.spot, s32[256,1]{1,0:T(8,128)S(1)} %get-tuple-element.12.slot_of, s32[256,1]{1,0:T(8,128)S(1)} %get-tuple-element.13.rank_of, s32[32,1]{1,0:T(8,128)S(1)} %get-tuple-element.14.own_slot, ...), custom_call_target="tpu_custom_call" | custom-call | tf_op jit(solution)/shard_map/attend/pallas_call | solution.py:307
  55.5 28.4 %all_to_all.15.parts = bf16[8,32,640]{2,1,0:T(8,128)(2,1)S(1)} all-to-all(bf16[8,32,640]{2,1,0:T(8,128)(2,1)S(1)} %get-tuple-element.15), channel_id=1, replica_groups={{0,64,128,192,256,320,384,448},{32,96,160,224,288,352,416,480},{1,65,12..., dimensions={0} | all-to-all | bytes 655360 | tf_op jit(solution)/shard_map/all_to_all | solution.py:336
  84.9 4.5 %all-to-all-start.1 = ((bf16[8,32,512]{2,1,0:T(8,128)(2,1)}), bf16[8,32,512]{2,1,0:T(8,128)(2,1)S(1)}, u32[]{:S(2)}, u32[]{:S(2)}) async-start(bf16[8,32,512]{2,1,0:T(8,128)(2,1)} %join.1), calls=%async_computation.1 | async-start | bytes 524288 | tf_op jit(solution)/shard_map/all_to_all | solution.py:345
  89.4 2.7 %collective-permute-start.10 = (bf16[1024,128]{1,0:T(8,128)(2,1)}, bf16[1024,128]{1,0:T(8,128)(2,1)S(1)}, u32[]{:S(2)}, u32[]{:S(2)}) collective-permute-start(bf16[1024,128]{1,0:T(8,128)(2,1)} %home.1), channel_id=1, source_target_pairs={{0,1},{1,0},{2,3},{3,2},{4,5},{5,4},{6,7},{7,6},{8,9},{9,8},{10,11... | collective-permute-start | bytes 786440 | tf_op jit(solution)/shard_map/ppermute | solution.py:21
  92.1 3.1 %collective-permute-start.11 = (bf16[1024,128]{1,0:T(8,128)(2,1)}, bf16[1024,128]{1,0:T(8,128)(2,1)S(1)}, u32[]{:S(2)}, u32[]{:S(2)}) collective-permute-start(bf16[1024,128]{1,0:T(8,128)(2,1)} %home.1), channel_id=1, source_target_pairs={{0,2},{1,3},{2,0},{3,1},{4,6},{5,7},{6,4},{7,5},{8,10},{9,11},{10,... | collective-permute-start | bytes 786440 | tf_op jit(solution)/shard_map/ppermute | solution.py:21
  95.2 4.6 %collective-permute-start.12 = (bf16[1024,128]{1,0:T(8,128)(2,1)}, bf16[1024,128]{1,0:T(8,128)(2,1)S(1)}, u32[]{:S(2)}, u32[]{:S(2)}) collective-permute-start(bf16[1024,128]{1,0:T(8,128)(2,1)} %home.1), channel_id=1, source_target_pairs={{0,3},{1,2},{2,1},{3,0},{4,7},{5,6},{6,5},{7,4},{8,11},{9,10},{10,... | collective-permute-start | bytes 786440 | tf_op jit(solution)/shard_map/ppermute | solution.py:21
  99.8 6.2 %all-to-all-done.1 = bf16[8,32,512]{2,1,0:T(8,128)(2,1)S(1)} async-done(((bf16[8,32,512]{2,1,0:T(8,128)(2,1)}), bf16[8,32,512]{2,1,0:T(8,128)(2,1)S(1)}, u32[]{:S(2)}, u32[]{:S(2)}) %all-to-all-start.1) | async-done | bytes 262176 | tf_op jit(solution)/shard_map/all_to_all | solution.py:345
  106.0 1.9 %collective-permute-start.9 = (bf16[256,512]{1,0:T(8,128)(2,1)S(1)}, bf16[256,512]{1,0:T(8,128)(2,1)S(1)}, u32[]{:S(2)}, u32[]{:S(2)}) collective-permute-start(bf16[256,512]{1,0:T(8,128)(2,1)S(1)} %bitcast.19), channel_id=1, source_target_pairs={{0,32},{32,0},{64,96},{96,64},{128,160},{160,128},{192,224},{224,1... | collective-permute-start | bytes 786440 | tf_op jit(solution)/shard_map/ppermute | solution.py:21
  107.9 2.1 %collective-permute-done.12.w3 = bf16[1024,128]{1,0:T(8,128)(2,1)S(1)} collective-permute-done((bf16[1024,128]{1,0:T(8,128)(2,1)}, bf16[1024,128]{1,0:T(8,128)(2,1)S(1)}, u32[]{:S(2)}, u32[]{:S(2)}) %collective-permute-start.12) | collective-permute-done | bytes 262176 | tf_op jit(solution)/shard_map/ppermute | solution.py:21
  111.9 15.8 %all_to_all.16.parts = bf16[16,128,128]{2,1,0:T(8,128)(2,1)S(1)} all-to-all(bf16[16,128,128]{2,1,0:T(8,128)(2,1)S(1)} %project.1), channel_id=1, replica_groups={{0,1,2,3,4,5,6,7,8,9,10,11,12,13,14,15},{16,17,18,19,20,21,22,23,24,25,..., dimensions={0} | all-to-all | bytes 1048576 | tf_op jit(solution)/shard_map/all_to_all | solution.py:359
  128.3 6.4 %collective-permute-start.13 = (bf16[128,128]{1,0:T(8,128)(2,1)S(1)}, bf16[128,128]{1,0:T(8,128)(2,1)S(1)}, u32[]{:S(2)}, u32[]{:S(2)}) collective-permute-start(bf16[128,128]{1,0:T(8,128)(2,1)S(1)} %get-tuple-element.18), channel_id=1, source_target_pairs={{0,16},{4,20},{8,24},{12,28},{16,0},{20,4},{24,8},{28,12},{1,17},{... | collective-permute-start | bytes 98312 | tf_op jit(solution)/shard_map/ppermute | solution.py:21
  134.7 8.2 %collective-permute-done.13 = bf16[128,128]{1,0:T(8,128)(2,1)S(1)} collective-permute-done((bf16[128,128]{1,0:T(8,128)(2,1)S(1)}, bf16[128,128]{1,0:T(8,128)(2,1)S(1)}, u32[]{:S(2)}, u32[]{:S(2)}) %collective-permute-start.13) | collective-permute-done | bytes 32800 | tf_op jit(solution)/shard_map/ppermute | solution.py:21
  (35 shorter events, 9.8 us)
Async XLA Ops:
  0.0 40.9 %copy-start.3 = (bf16[1,40,2,128]{3,2,1,0:T(2,128)(2,1)S(1)}, bf16[1,40,2,128]{3,2,1,0:T(2,128)(2,1)}, u32[]{:S(2)}) copy-start(bf16[1,40,2,128]{3,2,1,0:T(2,128)(2,1)} %param.13) | copy-start | bytes 61444
  0.0 48.6 %collective-permute-start.6 = (bf16[8,1024,128]{2,1,0:T(8,128)(2,1)}, bf16[8,1024,128]{2,1,0:T(8,128)(2,1)S(1)}, u32[]{:S(2)}, u32[]{:S(2)}) collective-permute-start(bf16[8,1024,128]{2,1,0:T(8,128)(2,1)} %bitcast.17), channel_id=1, source_target_pairs={{0,32},{32,0},{64,96},{96,64},{128,160},{160,128},{192,224},{224,1... | collective-permute-start | bytes 6291464 | tf_op jit(solution)/shard_map/ppermute | solution.py:21
  2.1 46.6 %collective-permute-start.7 = (bf16[8,1024,128]{2,1,0:T(8,128)(2,1)}, bf16[8,1024,128]{2,1,0:T(8,128)(2,1)}, u32[]{:S(2)}, u32[]{:S(2)}) collective-permute-start(bf16[8,1024,128]{2,1,0:T(8,128)(2,1)} %bitcast.21), channel_id=1, source_target_pairs={{0,32},{32,0},{64,96},{96,64},{128,160},{160,128},{192,224},{224,1... | collective-permute-start | bytes 6291464 | tf_op jit(solution)/shard_map/ppermute | solution.py:21
  5.3 15.1 %collective-permute-start = (bf16[40,512]{1,0:T(8,128)(2,1)S(1)}, bf16[40,512]{1,0:T(8,128)(2,1)S(1)}, u32[]{:S(2)}, u32[]{:S(2)}) collective-permute-start(bf16[40,512]{1,0:T(8,128)(2,1)S(1)} %get-tuple-element.21), channel_id=1, source_target_pairs={{0,32},{32,0},{64,96},{96,64},{128,160},{160,128},{192,224},{224,1... | collective-permute-start | bytes 122888 | tf_op jit(solution)/shard_map/ppermute | solution.py:21
  7.2 19.0 %collective-permute-start.2 = (bf16[40,512]{1,0:T(8,128)(2,1)S(1)}, bf16[40,512]{1,0:T(8,128)(2,1)S(1)}, u32[]{:S(2)}, u32[]{:S(2)}) collective-permute-start(bf16[40,512]{1,0:T(8,128)(2,1)S(1)} %get-tuple-element.21), channel_id=1, source_target_pairs={{0,288},{32,256},{64,352},{96,320},{128,416},{160,384},{192,480},{... | collective-permute-start | bytes 122888 | tf_op jit(solution)/shard_map/ppermute | solution.py:21
  16.4 9.8 %collective-permute-start.1 = (bf16[40,512]{1,0:T(8,128)(2,1)S(1)}, bf16[40,512]{1,0:T(8,128)(2,1)S(1)}, u32[]{:S(2)}, u32[]{:S(2)}) collective-permute-start(bf16[40,512]{1,0:T(8,128)(2,1)S(1)} %get-tuple-element.20), channel_id=1, source_target_pairs={{0,256},{32,288},{64,320},{96,352},{128,384},{160,416},{192,448},{... | collective-permute-start | bytes 122888 | tf_op jit(solution)/shard_map/ppermute | solution.py:21
  20.4 25.2 %collective-permute-start.8 = (bf16[2064,128]{1,0:T(8,128)(2,1)S(1)}, bf16[2064,128]{1,0:T(8,128)(2,1)S(1)}, u32[]{:S(2)}, u32[]{:S(2)}) collective-permute-start(bf16[2064,128]{1,0:T(8,128)(2,1)S(1)} %maximum_maximum_fusion.suf), channel_id=1, source_target_pairs={{0,32},{32,0},{64,96},{96,64},{128,160},{160,128},{192,224},{224,1... | collective-permute-start | bytes 1585160 | tf_op jit(solution)/shard_map/ppermute | solution.py:21
  26.3 11.9 %collective-permute-start.3 = (bf16[160,512]{1,0:T(8,128)(2,1)S(1)}, bf16[160,512]{1,0:T(8,128)(2,1)S(1)}, u32[]{:S(2)}, u32[]{:S(2)}) collective-permute-start(bf16[160,512]{1,0:T(8,128)(2,1)S(1)} %pad_maximum_fusion), channel_id=1, source_target_pairs={{0,128},{32,160},{64,192},{96,224},{128,0},{160,32},{192,64},{224,... | collective-permute-start | bytes 491528 | tf_op jit(solution)/shard_map/ppermute | solution.py:21
  38.2 10.4 %collective-permute-start.4 = (bf16[320,512]{1,0:T(8,128)(2,1)S(1)}, bf16[320,512]{1,0:T(8,128)(2,1)}, u32[]{:S(2)}, u32[]{:S(2)}) collective-permute-start(bf16[320,512]{1,0:T(8,128)(2,1)S(1)} %constant_dynamic-update-slice_fusion.near), channel_id=1, source_target_pairs={{0,64},{32,96},{64,0},{96,32},{128,192},{160,224},{192,128},{224,1... | collective-permute-start | bytes 983048 | tf_op jit(solution)/shard_map/ppermute | solution.py:21
  40.9 4.7 %collective-permute-start.5 = (bf16[56,256]{1,0:T(8,128)(2,1)S(1)}, bf16[56,256]{1,0:T(8,128)(2,1)S(1)}, u32[]{:S(2)}, u32[]{:S(2)}) collective-permute-start(bf16[56,256]{1,0:T(8,128)(2,1)S(1)} %pad.4.small), channel_id=1, source_target_pairs={{0,32},{32,0},{64,96},{96,64},{128,160},{160,128},{192,224},{224,1... | collective-permute-start | bytes 86024 | tf_op jit(solution)/shard_map/ppermute | solution.py:21
  42.9 1.8 %copy-start.1 = (s32[1,256]{1,0:T(1,128)S(1)}, s32[1,256]{1,0:T(1,128)}, u32[]{:S(2)}) copy-start(s32[1,256]{1,0:T(1,128)} %prompt.1) | copy-start | bytes 3076
  42.9 1.8 %copy-start.2 = (s32[1,16]{1,0:T(1,128)S(1)}, s32[1,16]{1,0:T(1,128)}, u32[]{:S(2)}) copy-start(s32[1,16]{1,0:T(1,128)} %counts.1) | copy-start | bytes 196
  42.9 5.7 %copy-start = (bf16[1,8,1024,128]{3,2,1,0:T(8,128)(2,1)S(1)}, bf16[1,8,1024,128]{3,2,1,0:T(8,128)(2,1)}, u32[]{:S(2)}) copy-start(bf16[1,8,1024,128]{3,2,1,0:T(8,128)(2,1)} %param.14) | copy-start | bytes 6291460
  84.9 21.1 %all-to-all-start.1 = ((bf16[8,32,512]{2,1,0:T(8,128)(2,1)}), bf16[8,32,512]{2,1,0:T(8,128)(2,1)S(1)}, u32[]{:S(2)}, u32[]{:S(2)}) async-start(bf16[8,32,512]{2,1,0:T(8,128)(2,1)} %join.1), calls=%async_computation.1 | async-start | bytes 524288 | tf_op jit(solution)/shard_map/all_to_all | solution.py:345
  89.4 18.5 %collective-permute-start.10 = (bf16[1024,128]{1,0:T(8,128)(2,1)}, bf16[1024,128]{1,0:T(8,128)(2,1)S(1)}, u32[]{:S(2)}, u32[]{:S(2)}) collective-permute-start(bf16[1024,128]{1,0:T(8,128)(2,1)} %home.1), channel_id=1, source_target_pairs={{0,1},{1,0},{2,3},{3,2},{4,5},{5,4},{6,7},{7,6},{8,9},{9,8},{10,11... | collective-permute-start | bytes 786440 | tf_op jit(solution)/shard_map/ppermute | solution.py:21
  92.1 15.8 %collective-permute-start.11 = (bf16[1024,128]{1,0:T(8,128)(2,1)}, bf16[1024,128]{1,0:T(8,128)(2,1)S(1)}, u32[]{:S(2)}, u32[]{:S(2)}) collective-permute-start(bf16[1024,128]{1,0:T(8,128)(2,1)} %home.1), channel_id=1, source_target_pairs={{0,2},{1,3},{2,0},{3,1},{4,6},{5,7},{6,4},{7,5},{8,10},{9,11},{10,... | collective-permute-start | bytes 786440 | tf_op jit(solution)/shard_map/ppermute | solution.py:21
  95.2 14.9 %collective-permute-start.12 = (bf16[1024,128]{1,0:T(8,128)(2,1)}, bf16[1024,128]{1,0:T(8,128)(2,1)S(1)}, u32[]{:S(2)}, u32[]{:S(2)}) collective-permute-start(bf16[1024,128]{1,0:T(8,128)(2,1)} %home.1), channel_id=1, source_target_pairs={{0,3},{1,2},{2,1},{3,0},{4,7},{5,6},{6,5},{7,4},{8,11},{9,10},{10,... | collective-permute-start | bytes 786440 | tf_op jit(solution)/shard_map/ppermute | solution.py:21
  106.0 4.1 %collective-permute-start.9 = (bf16[256,512]{1,0:T(8,128)(2,1)S(1)}, bf16[256,512]{1,0:T(8,128)(2,1)S(1)}, u32[]{:S(2)}, u32[]{:S(2)}) collective-permute-start(bf16[256,512]{1,0:T(8,128)(2,1)S(1)} %bitcast.19), channel_id=1, source_target_pairs={{0,32},{32,0},{64,96},{96,64},{128,160},{160,128},{192,224},{224,1... | collective-permute-start | bytes 786440 | tf_op jit(solution)/shard_map/ppermute | solution.py:21
  128.3 14.6 %collective-permute-start.13 = (bf16[128,128]{1,0:T(8,128)(2,1)S(1)}, bf16[128,128]{1,0:T(8,128)(2,1)S(1)}, u32[]{:S(2)}, u32[]{:S(2)}) collective-permute-start(bf16[128,128]{1,0:T(8,128)(2,1)S(1)} %get-tuple-element.18), channel_id=1, source_target_pairs={{0,16},{4,20},{8,24},{12,28},{16,0},{20,4},{24,8},{28,12},{1,17},{... | collective-permute-start | bytes 98312 | tf_op jit(solution)/shard_map/ppermute | solution.py:21
